TPU v7x, 32 devices: a whole 2x2x4 slice. The times are simulated.
32 devices in a mesh: row: 4 (over y, x), col: 8 (over z, core).
Axes of the slice: x: 2, y: 2, z: 4, core: 2. Of those that a mesh axis runs over, the one named last changes fastest.
Arguments:
- leaf_state_map: bfloat16 [128, 512, 512], P(('row', 'col')), may hold values from -0.1875 to 0.1875
- leaf_input_map: bfloat16 [128, 512, 256], P(('row', 'col')), may hold values from -0.25 to 0.25
- leaf_weight: bfloat16 [128], P(('row', 'col')), may hold values from 0.29882812 to 3
- leaf_count: int32 [32], P(('row', 'col')), may hold values from 1 to 4, as said below
- mid_state_map: bfloat16 [32, 512, 512], P(('row', 'col')), may hold values from -0.1875 to 0.1875
- mid_input_map: bfloat16 [32, 512, 256], P(('row', 'col')), may hold values from -0.25 to 0.25
- mid_weight: float32 [32], P(('row', 'col')), may hold values from 0.3 to 3
- mid_parent: int32 [32], P(('row', 'col')), may hold values from 0 to 1, as said below
- up_state_map: bfloat16 [8, 512, 512], P('row'), may hold values from -0.1875 to 0.1875
- up_input_map: bfloat16 [8, 512, 256], P('row'), may hold values from -0.25 to 0.25
- up_weight: float32 [8], P('row'), may hold values from 0.3 to 3
- root_cov: bfloat16 [512, 512], replicated, as said below
- state_cost: float32 [512], replicated, may hold values from 0.3 to 3
- control_cost: float32 [256], replicated, may hold values from 0.3 to 3
- noise_cov: float32 [512], replicated, may hold values from 0.05 to 0.5
Outputs:
- root_gain: bfloat16 [256, 512], replicated
- root_value: bfloat16 [512, 512], replicated
- up_gain: bfloat16 [8, 256, 512], P('row')
- up_value: bfloat16 [8, 512, 512], P('row')
- up_cov: bfloat16 [8, 512, 512], P('row')
- mid_gain: bfloat16 [32, 256, 512], P(('row', 'col'))
- mid_value: bfloat16 [32, 512, 512], P(('row', 'col'))
- mid_cov: bfloat16 [32, 512, 512], P(('row', 'col'))
- leaf_cov: bfloat16 [128, 512, 512], P(('row', 'col'))
Inputs may be any that keep to these rules, and one draw needn't show every extreme that they name: `leaf_count`: the number of live leaves of each section-2 node; some node has 4 in every draw. `mid_parent`: the parent slot of each section-2 node within its row group; every section-1 node has at least one child. `root_cov`: symmetric positive definite.
All inputs are finite; a program needn't handle non-finite values.
Results may differ from a plain program's by a relative error of at most 0.02.
Values may be sent and summed in bfloat16 or wider, within the bound.
No kernel may reach another device: no remote copies, remote signals or barrier semaphores. Data moves between devices by JAX's collectives and lax.ppermute only.
A program may use at most 128 MiB of HBM per device.

v0:
```python
import functools

import jax
import jax.numpy as jnp
from jax import lax
from jax.experimental import pallas as pl
from jax.experimental.pallas import tpu as pltpu
from jax.sharding import PartitionSpec as P

NX = 512
NU = 256
S1_ROW = 2
T = 128
HT = T // 2
WROWS = 16

f32 = jnp.float32
bf16 = jnp.bfloat16

BB_BLOCKS = ((0, 0), (1, 0), (1, 1))
BA_BLOCKS = tuple((i, j) for i in range(2) for j in range(4))
AA_BLOCKS = tuple((i, j) for i in range(4) for j in range(i + 1))
FIRST = len(BB_BLOCKS) + len(BA_BLOCKS)
SECOND = len(AA_BLOCKS)
ROWS1 = FIRST * HT + WROWS
ROWS2 = SECOND * HT

NN = (((1,), (0,)), ((), ()))
NT = (((1,), (1,)), ((), ()))
TN = (((0,), (0,)), ((), ()))


def dot(a, b, dims=NN):
    return lax.dot_general(a, b, dims, preferred_element_type=f32)


def split(x):
    high = x.astype(bf16)
    return high, (x - high.astype(f32)).astype(bf16)


def dot3(a, b, dims=NN):
    a_high, a_low = split(a)
    b_high, b_low = split(b)
    return dot(a_high, b_high, dims) + (dot(a_high, b_low, dims) + dot(a_low, b_high, dims))


def tree_sum(terms):
    while len(terms) > 1:
        terms = [terms[i] + terms[i + 1] for i in range(0, len(terms), 2)]
    return terms[0]


def row_of(x, k):
    return jnp.broadcast_to(x[k : k + 1, :], (8, T))


def column_of(x, k):
    return jnp.broadcast_to(x[:, k : k + 1], (8, T))


def negative_inverse(blocks):
    count = len(blocks)
    lane = lax.broadcasted_iota(jnp.int32, (8, T), 1)
    sub = lax.broadcasted_iota(jnp.int32, (8, T), 0)

    def pivot(block, first):
        cols = [column_of(block, first + k) for k in range(8)]
        for k in range(8):
            here = sub == k
            inverse = 1.0 / row_of(cols[k], k)
            lead = jnp.where(here, -1.0, cols[k])
            cols = [
                lead * inverse
                if j == k
                else jnp.where(here, 0.0, cols[j]) - lead * (row_of(cols[j], k) * inverse)
                for j in range(8)
            ]
        inside = (lane >= first) & (lane < first + 8)
        rows = jnp.where(inside, jnp.where(lane - first == sub, -1.0, 0.0), block)
        return tree_sum([cols[j] * row_of(rows, j) for j in range(8)])

    def update(block, lead, first):
        inside = (lane >= first) & (lane < first + 8)
        added = tree_sum([column_of(block, first + k) * row_of(lead, k) for k in range(8)])
        return jnp.where(inside, 0.0, block) + added

    blocks = list(blocks)
    waiting = None
    for i in range(count):
        if waiting is not None and i + 1 < count:
            blocks[i + 1] = update(blocks[i + 1], waiting, 8 * (i - 1))
        lead = pivot(blocks[i], 8 * i)
        if i + 1 < count:
            blocks[i + 1] = update(blocks[i + 1], lead, 8 * i)
        for t in range(count):
            if waiting is not None and t not in (i - 1, i, i + 1):
                blocks[t] = update(blocks[t], waiting, 8 * (i - 1))
        blocks[i] = -lead
        waiting = lead
    last = count - 1
    return [
        blocks[t] if t == last else update(blocks[t], waiting, 8 * last) for t in range(count)
    ]


def invert(source, target):
    rows = negative_inverse([source[8 * i : 8 * i + 8, :] for i in range(T // 8)])
    for i, row in enumerate(rows):
        target[8 * i : 8 * i + 8, :] = -row


def diagonal(block, costs_row):
    i = lax.broadcasted_iota(jnp.int32, block.shape, 0)
    j = lax.broadcasted_iota(jnp.int32, block.shape, 1)
    return block + jnp.where(i == j, jnp.broadcast_to(costs_row, block.shape), 0.0)


def riccati(bb, ba, aa, state_cost, control_cost, hess, inv_a, inv_s, gain, value):
    hess[...] = diagonal(bb(0, 0), control_cost[0:1, :])
    invert(hess, inv_a)
    h21 = bb(1, 0)
    first_inv = inv_a[...]
    through = dot3(h21, first_inv)
    through_t = dot3(first_inv, h21, NT)
    hess[...] = diagonal(bb(1, 1), control_cost[1:2, :]) - dot3(through, h21, NT)
    invert(hess, inv_s)
    block_ba = ba()
    top, bottom = block_ba[:T, :], block_ba[T:, :]
    below = dot3(inv_s[...], bottom - dot3(through, top))
    above = dot3(first_inv, top) - dot3(through_t, below)
    feedback = -jnp.concatenate([above, below], axis=0)
    gain[...] = feedback.astype(bf16)
    for half in range(2):
        width = NU * (half + 1)
        rows = dot3(block_ba[:, NU * half : NU * half + NU], feedback[:, :width], TN)
        for bi in range(2):
            i = 2 * half + bi
            for j in range(i + 1):
                item = aa(i, j) + rows[T * bi : T * bi + T, T * j : T * j + T]
                if i == j:
                    item = diagonal(item, state_cost[i : i + 1, :])
                else:
                    value[T * j : T * j + T, T * i : T * i + T] = item.T.astype(bf16)
                value[T * i : T * i + T, T * j : T * j + T] = item.astype(bf16)


def lower_terms(states, inputs, applied):
    return (
        dot(inputs[...], applied[...], TN),
        dot(states[:, NU:], applied[:, :NX], TN),
        dot(states[:, :NU], applied[:, :NU], TN),
    )


def blocks_of(parts):
    b_rows, a_high, a_low = parts
    for n, (i, j) in enumerate(BB_BLOCKS):
        yield 0, n, b_rows[T * i : T * i + T, NX + T * j : NX + T * j + T]
    for n, (i, j) in enumerate(BA_BLOCKS):
        yield 0, len(BB_BLOCKS) + n, b_rows[T * i : T * i + T, T * j : T * j + T]
    for n, (i, j) in enumerate(AA_BLOCKS):
        source = a_low if i < 2 else a_high
        yield 1, n, source[T * (i % 2) : T * (i % 2) + T, T * j : T * j + T]


def pack(parts, scale, weight_rows, out1, out2):
    outs = (out1, out2)
    for chunk, n, block in blocks_of(parts):
        scaled = (scale * block).astype(bf16)
        for h in range(2):
            outs[chunk][h, HT * n : HT * n + HT, :] = scaled[HT * h : HT * h + HT, :]
    for h in range(2):
        out1[h, HT * FIRST :, :] = weight_rows


def spread_weight(weight, place):
    lane = lax.broadcasted_iota(jnp.int32, (WROWS, T), 1)
    sub = lax.broadcasted_iota(jnp.int32, (WROWS, T), 0)
    full = jnp.full((WROWS, T), weight, f32)
    high = full.astype(bf16).astype(f32)
    item = jnp.where(sub == 0, high, jnp.where(sub == 1, full - high, 0.0))
    return jnp.where(lane == place, item, 0.0).astype(bf16)


def unpack(mine1, other1, mine2, other2, which, sums):
    weight = jnp.sum(mine1[HT * FIRST :, :].astype(f32))
    scale = 1.0 / jnp.full((HT, T), weight, f32)
    swap = jnp.full((HT, T), which, jnp.int32) == 1
    for n in range(FIRST + SECOND):
        mine, other = (mine1, other1) if n < FIRST else (mine2, other2)
        at = HT * (n if n < FIRST else n - FIRST)
        a = mine[at : at + HT, :].astype(f32) * scale
        b = other[at : at + HT, :].astype(f32) * scale
        sums[n, :HT, :] = jnp.where(swap, b, a)
        sums[n, HT:, :] = jnp.where(swap, a, b)


def riccati_packed(sums, state_cost, control_cost, scratch, gain, value):
    riccati(
        lambda i, j: sums[BB_BLOCKS.index((i, j))],
        lambda: jnp.concatenate(
            [
                jnp.concatenate([sums[len(BB_BLOCKS) + 4 * i + j] for j in range(4)], axis=1)
                for i in range(2)
            ],
            axis=0,
        ),
        lambda i, j: sums[FIRST + AA_BLOCKS.index((i, j))],
        state_cost,
        control_cost,
        *scratch,
        gain,
        value,
    )


def apply_value(value, states, inputs, applied):
    applied[:, :NX] = dot(value[...], states[...]).astype(bf16)
    applied[:, NX:] = dot(value[...], inputs[...]).astype(bf16)


def lower_kernel(
    scalars, leaf_state, leaf_input, mid_state, mid_input, state_cost, control_cost,
    gain, value, out1, out2,
    cost_cols, applied, acc_b, acc_high, acc_low, hess, inv_a, inv_s,
):
    slot = pl.program_id(0)
    slots = pl.num_programs(0)
    live = scalars[1].astype(jnp.int32)

    @pl.when(slot == 0)
    def _():
        for i in range(NX // T):
            cost_cols[T * i : T * i + T, :] = jnp.broadcast_to(state_cost[i : i + 1, :], (T, T)).T
        acc_b[...] = jnp.zeros_like(acc_b)
        acc_high[...] = jnp.zeros_like(acc_high)
        acc_low[...] = jnp.zeros_like(acc_low)

    @pl.when(slot < live)
    def _():
        weight = scalars[4 + slot]
        cost = cost_cols[...]
        for j in range(NX // T):
            applied[:, T * j : T * j + T] = (
                cost * leaf_state[:, T * j : T * j + T].astype(f32)
            ).astype(bf16)
        for j in range(NU // T):
            applied[:, NX + T * j : NX + T * j + T] = (
                cost * leaf_input[:, T * j : T * j + T].astype(f32)
            ).astype(bf16)
        for acc, part in zip(
            (acc_b, acc_high, acc_low), lower_terms(leaf_state, leaf_input, applied)
        ):
            acc[...] += weight * part

    @pl.when(slot == slots - 1)
    def _():
        total = lax.fori_loop(
            0, live, lambda n, running: running + scalars[4 + n], jnp.float32(0.0)
        )
        mean_b = 1.0 / jnp.full((T, T), total, f32)
        scale = 1.0 / jnp.full((NU, NX), total, f32)
        riccati(
            lambda i, j: acc_b[T * i : T * i + T, NX + T * j : NX + T * j + T] * mean_b,
            lambda: acc_b[:, :NX] * scale,
            lambda i, j: (acc_low if i < 2 else acc_high)[
                T * (i % 2) : T * (i % 2) + T, T * j : T * j + T
            ]
            * mean_b,
            state_cost,
            control_cost,
            hess,
            inv_a,
            inv_s,
            gain,
            value,
        )
        apply_value(value, mid_state, mid_input, applied)
        pack(
            lower_terms(mid_state, mid_input, applied),
            scalars[0],
            spread_weight(scalars[0], scalars[2].astype(jnp.int32)),
            out1,
            out2,
        )


def upper_kernel(
    which, scalars, mine1, other1, mine2, other2, up_state, up_input, state_cost, control_cost,
    gain, value, out1, out2,
    sums, applied, hess, inv_a, inv_s,
):
    unpack(mine1, other1, mine2, other2, which[0], sums)
    riccati_packed(sums, state_cost, control_cost, (hess, inv_a, inv_s), gain, value)
    slot = which[1]
    states = up_state.at[slot]
    inputs = up_input.at[slot]
    apply_value(value, states, inputs, applied)
    pack(
        lower_terms(states, inputs, applied),
        scalars[0],
        spread_weight(scalars[0], which[2]),
        out1,
        out2,
    )


def propagate(parent_cov, gain, states, inputs, noise_cov, closed, moved, target):
    closed[...] = (states[...].astype(f32) + dot(inputs[...], gain[...])).astype(bf16)
    moved[...] = dot(closed[...], parent_cov[...]).astype(bf16)
    for i in range(NX // T):
        rows = dot(moved[T * i : T * i + T, :], closed[...], NT)
        for j in range(NX // T):
            item = rows[:, T * j : T * j + T]
            if i == j:
                item = diagonal(item, noise_cov[i : i + 1, :])
            target[T * i : T * i + T, T * j : T * j + T] = item.astype(bf16)


def root_kernel(
    which, mine1, other1, mine2, other2, state_cost, control_cost, noise_cov, root_cov,
    up_state, up_input, mid_state, mid_input, leaf_state, leaf_input, parent_gain, mid_gain,
    gain, value, up_cov, mid_cov, leaf_cov,
    sums, hess, inv_a, inv_s, closed, moved,
):
    unpack(mine1, other1, mine2, other2, which[0], sums)
    riccati_packed(sums, state_cost, control_cost, (hess, inv_a, inv_s), gain, value)

    for slot in range(up_state.shape[0]):
        propagate(
            root_cov, gain, up_state.at[slot], up_input.at[slot], noise_cov, closed, moved,
            up_cov.at[slot],
        )
    propagate(
        up_cov.at[which[1]], parent_gain, mid_state, mid_input, noise_cov, closed, moved, mid_cov
    )

    @pl.loop(0, leaf_state.shape[0])
    def _(slot):
        @pl.when(slot < which[2])
        def _():
            propagate(
                mid_cov, mid_gain, leaf_state.at[slot], leaf_input.at[slot], noise_cov, closed,
                moved, leaf_cov.at[slot],
            )

        @pl.when(slot >= which[2])
        def _():
            leaf_cov[slot, :, :] = jnp.zeros((NX, NX), bf16)


SMEM = pl.BlockSpec(memory_space=pltpu.SMEM)
VMEM = pl.BlockSpec(memory_space=pltpu.VMEM)
LIMIT = pltpu.CompilerParams(vmem_limit_bytes=56 << 20)


def matrix(*shape, kind=bf16):
    return jax.ShapeDtypeStruct(shape, kind)


SQUARES = [pltpu.VMEM((T, T), f32)] * 3


def local(
    n_row,
    n_col,
    leaf_state_map,
    leaf_input_map,
    leaf_weight,
    leaf_count,
    mid_state_map,
    mid_input_map,
    mid_weight,
    mid_parent,
    up_state_map,
    up_input_map,
    up_weight,
    root_cov,
    state_cost,
    control_cost,
    noise_cov,
):
    slots = leaf_state_map.shape[0]
    row = lax.axis_index("row")
    col = lax.axis_index("col")
    core = col % 2
    depth = col // 2
    state_rows = state_cost.reshape(NX // T, T)
    control_rows = control_cost.reshape(NU // T, T)
    noise_rows = noise_cov.reshape(NX // T, T)
    parent = mid_parent[0]

    scalars = jnp.concatenate(
        [
            mid_weight,
            leaf_count.astype(f32),
            col.astype(f32)[None],
            jnp.zeros((1,), f32),
            leaf_weight.astype(f32),
        ]
    )
    mid_gain, mid_value, first, second = pl.pallas_call(
        lower_kernel,
        grid=(slots,),
        out_shape=(
            matrix(NU, NX),
            matrix(NX, NX),
            matrix(2, ROWS1, T),
            matrix(2, ROWS2, T),
        ),
        in_specs=[
            SMEM,
            pl.BlockSpec((None, NX, NX), lambda n: (n, 0, 0)),
            pl.BlockSpec((None, NX, NU), lambda n: (n, 0, 0)),
            VMEM,
            VMEM,
            VMEM,
            VMEM,
        ],
        out_specs=(VMEM,) * 4,
        scratch_shapes=[
            pltpu.VMEM((NX, T), f32),
            pltpu.VMEM((NX, NX + NU), bf16),
            pltpu.VMEM((NU, NX + NU), f32),
            pltpu.VMEM((NU, NX), f32),
            pltpu.VMEM((NU, NU), f32),
            *SQUARES,
        ],
        compiler_params=LIMIT,
        name="lower",
    )(
        scalars,
        leaf_state_map,
        leaf_input_map,
        mid_state_map[0],
        mid_input_map[0],
        state_rows,
        control_rows,
    )

    def across(x, flip):
        return lax.ppermute(x, "col", [(i, i ^ flip) for i in range(n_col)])

    def select(flag, a, b):
        return jnp.where(flag, a, b)

    zero = jnp.zeros((), bf16)
    half = depth % 2
    other_parent = lax.ppermute(
        parent.astype(f32).reshape(1, 1), "col", [(i, i ^ 1) for i in range(n_col)]
    )[0, 0]
    own_flag = parent == core
    other_flag = other_parent == core.astype(f32)

    def reduce_col(x):
        y = across(x, 1)
        both = select(own_flag, x, zero).astype(f32) + select(other_flag, y, zero).astype(f32)
        both = both.astype(bf16)
        kept = select(half == 0, both[0], both[1])
        sent = select(half == 0, both[1], both[0])
        kept = kept + across(sent, 2)
        flip = 4
        while flip < n_col:
            kept = kept + across(kept, flip)
            flip = flip * 2
        return kept, across(kept, 2)

    first_mine, first_other = reduce_col(first)
    second_mine, second_other = reduce_col(second)

    up_gain_own, up_value_own, first, second = pl.pallas_call(
        upper_kernel,
        out_shape=(
            matrix(NU, NX),
            matrix(NX, NX),
            matrix(2, ROWS1, T),
            matrix(2, ROWS2, T),
        ),
        in_specs=[SMEM, SMEM] + [VMEM] * 8,
        out_specs=(VMEM,) * 4,
        scratch_shapes=[
            pltpu.VMEM((FIRST + SECOND, T, T), f32),
            pltpu.VMEM((NX, NX + NU), bf16),
            *SQUARES,
        ],
        compiler_params=LIMIT,
        name="upper",
    )(
        jnp.stack([half, core, row * 2 + core]).astype(jnp.int32),
        lax.dynamic_slice(up_weight, (core,), (1,)),
        first_mine,
        first_other,
        second_mine,
        second_other,
        up_state_map,
        up_input_map,
        state_rows,
        control_rows,
    )
    up_gain_other = across(up_gain_own, 1)
    up_value_other = across(up_value_own, 1)
    is_low = core == 0
    up_gain = jnp.stack(
        [select(is_low, up_gain_own, up_gain_other), select(is_low, up_gain_other, up_gain_own)]
    )
    up_value = jnp.stack(
        [select(is_low, up_value_own, up_value_other), select(is_low, up_value_other, up_value_own)]
    )
    parent_gain = select(own_flag, up_gain_own, up_gain_other)

    row_bits = n_row.bit_length() - 1

    def along(x, step):
        bits = (step % row_bits, (step + row_bits // 2) % row_bits)
        return lax.ppermute(
            x,
            ("row", "col"),
            [
                (r * n_col + c, (r ^ (1 << bits[c % 2])) * n_col + c)
                for r in range(n_row)
                for c in range(n_col)
            ],
        )

    def reduce_row(x):
        kept = select(is_low, x[0], x[1])
        sent = select(is_low, x[1], x[0])
        kept = kept + across(sent, 1)
        for step in range(row_bits):
            kept = kept + along(kept, step)
        return kept, across(kept, 1)

    first_mine, first_other = reduce_row(first)
    second_mine, second_other = reduce_row(second)

    root_gain, root_value, up_cov, mid_cov, leaf_cov = pl.pallas_call(
        root_kernel,
        out_shape=(
            matrix(NU, NX),
            matrix(NX, NX),
            matrix(S1_ROW, NX, NX),
            matrix(NX, NX),
            matrix(slots, NX, NX),
        ),
        in_specs=[SMEM] + [VMEM] * 16,
        out_specs=(VMEM,) * 5,
        scratch_shapes=[
            pltpu.VMEM((FIRST + SECOND, T, T), f32),
            *SQUARES,
            pltpu.VMEM((NX, NX), bf16),
            pltpu.VMEM((NX, NX), bf16),
        ],
        compiler_params=LIMIT,
        name="root",
    )(
        jnp.stack([core, parent, leaf_count[0]]).astype(jnp.int32),
        first_mine,
        first_other,
        second_mine,
        second_other,
        state_rows,
        control_rows,
        noise_rows,
        root_cov,
        up_state_map,
        up_input_map,
        mid_state_map[0],
        mid_input_map[0],
        leaf_state_map,
        leaf_input_map,
        parent_gain,
        mid_gain,
    )
    return (
        root_gain,
        root_value,
        up_gain,
        up_value,
        up_cov,
        mid_gain[None],
        mid_value[None],
        mid_cov[None],
        leaf_cov,
    )


def solution(mesh):
    both = P(("row", "col"), None, None)
    flat = P(("row", "col"))
    up = P("row", None, None)
    return jax.shard_map(
        functools.partial(local, mesh.shape["row"], mesh.shape["col"]),
        mesh=mesh,
        in_specs=(
            both, both, flat, flat, both, both, flat, flat, up, up, P("row"), P(), P(), P(), P(),
        ),
        out_specs=(P(), P(), up, up, up, both, both, both, both),
        check_vma=False,
    )
```

profile of v0, /device:TPU:0, one launch (start us, length us, event | category | flops | bytes accessed | tf_op | source)
XLA Modules:
  0.0 115.7 jit_solution(7094126140556217434)
XLA Ops:
  1.9 1.3 %concatenate.3.scalars = f32[8]{0:T(128)} concatenate(f32[1]{0:T(128)S(6)} %copy.25, f32[1]{0:T(128)S(6)} %convert_element_type.33, f32[1]{0:T(128)} %bitcast.4, f32[1]{0:T(128)} %constant.39.clone.1, bf16[4]{0:T(256)(128)(2,1)} %param.17), dimensions={0} | concatenate | bytes 56 | tf_op jit(solution)/shard_map/concatenate | solution.py:394
  3.2 15.7 %lower.1 = (bf16[256,512]{1,0:T(8,128)(2,1)}, bf16[512,512]{1,0:T(8,128)(2,1)}, bf16[2,720,128]{2,1,0:T(8,128)(2,1)}, bf16[2,640,128]{2,1,0:T(8,128)(2,1)}) custom-call(f32[8]{0:T(128)} %concatenate.3.scalars, bf16[4,512,512]{2,1,0:T(8,128)(2,1)} %leaf_state.3, bf16[4,512,256]{2,1,0:T(8,128)(2,1)} %leaf_input.3, bf16[512,512]{1,0:T(8,128)(2,1)} %bitcast.41, ...), custom_call_target="tpu_custom_call" | custom-call | tf_op jit(solution)/shard_map/lower/pallas_call | solution.py:403
  18.9 0.5 collective-permute-start.5
  19.4 0.1 collective-permute-start.1
  20.1 1.3 %collective-permute-start = (f32[1,1]{1,0:T(1,128)}, f32[1,1]{1,0:T(1,128)}, u32[]{:S(2)}, u32[]{:S(2)}) collective-permute-start(f32[1,1]{1,0:T(1,128)} %bitcast.9), channel_id=1, source_target_pairs={{0,1},{1,0},{2,3},{3,2},{4,5},{5,4},{6,7},{7,6},{8,9},{9,8},{10,11... | collective-permute-start | bytes 20 | tf_op jit(solution)/shard_map/ppermute | solution.py:450
  22.0 0.0 collective-permute-done.5
  22.0 1.1 add_convert_fusion.1
  23.2 0.0 copy-start.10
  23.2 0.0 collective-permute-done.1
  23.2 1.1 add_convert_fusion
  24.4 1.7 %collective-permute-start.2 = (bf16[720,128]{1,0:T(8,128)(2,1)S(1)}, bf16[720,128]{1,0:T(8,128)(2,1)S(1)}, u32[]{:S(2)}, u32[]{:S(2)}) collective-permute-start(bf16[720,128]{1,0:T(8,128)(2,1)S(1)} %select_bitcast_fusion.5), channel_id=1, source_target_pairs={{0,2},{1,3},{2,0},{3,1},{4,6},{5,7},{6,4},{7,5},{8,10},{9,11},{10,... | collective-permute-start | bytes 552968 | tf_op jit(solution)/shard_map/ppermute | solution.py:443
  26.1 0.5 collective-permute-start.6
  26.5 4.2 %collective-permute-done.2 = bf16[720,128]{1,0:T(8,128)(2,1)S(1)} collective-permute-done((bf16[720,128]{1,0:T(8,128)(2,1)S(1)}, bf16[720,128]{1,0:T(8,128)(2,1)S(1)}, u32[]{:S(2)}, u32[]{:S(2)}) %collective-permute-start.2) | collective-permute-done | bytes 184352 | tf_op jit(solution)/shard_map/ppermute | solution.py:443
  30.8 5.8 %collective-permute-start.3 = (bf16[720,128]{1,0:T(8,128)(2,1)S(1)}, bf16[720,128]{1,0:T(8,128)(2,1)S(1)}, u32[]{:S(2)}, u32[]{:S(2)}) collective-permute-start(bf16[720,128]{1,0:T(8,128)(2,1)S(1)} %bitcast_add_fusion.1), channel_id=1, source_target_pairs={{0,4},{1,5},{2,6},{3,7},{4,0},{5,1},{6,2},{7,3},{8,12},{9,13},{10,... | collective-permute-start | bytes 552968 | tf_op jit(solution)/shard_map/ppermute | solution.py:443
  36.6 0.0 collective-permute-done.6
  36.6 3.5 %collective-permute-start.7 = (bf16[640,128]{1,0:T(8,128)(2,1)S(1)}, bf16[640,128]{1,0:T(8,128)(2,1)S(1)}, u32[]{:S(2)}, u32[]{:S(2)}) collective-permute-start(bf16[640,128]{1,0:T(8,128)(2,1)S(1)} %bitcast_add_fusion.3), channel_id=1, source_target_pairs={{0,4},{1,5},{2,6},{3,7},{4,0},{5,1},{6,2},{7,3},{8,12},{9,13},{10,... | collective-permute-start | bytes 491528 | tf_op jit(solution)/shard_map/ppermute | solution.py:443
  40.1 9.4 %collective-permute-done.3 = bf16[720,128]{1,0:T(8,128)(2,1)S(1)} collective-permute-done((bf16[720,128]{1,0:T(8,128)(2,1)S(1)}, bf16[720,128]{1,0:T(8,128)(2,1)S(1)}, u32[]{:S(2)}, u32[]{:S(2)}) %collective-permute-start.3) | collective-permute-done | bytes 184352 | tf_op jit(solution)/shard_map/ppermute | solution.py:443
  49.6 0.1 add.56.mine1
  49.6 0.0 copy-start
  49.6 0.1 collective-permute-start.4
  49.7 2.1 %collective-permute-done.7 = bf16[640,128]{1,0:T(8,128)(2,1)S(1)} collective-permute-done((bf16[640,128]{1,0:T(8,128)(2,1)S(1)}, bf16[640,128]{1,0:T(8,128)(2,1)S(1)}, u32[]{:S(2)}, u32[]{:S(2)}) %collective-permute-start.7) | collective-permute-done | bytes 163872 | tf_op jit(solution)/shard_map/ppermute | solution.py:443
  51.9 0.0 copy-start.2
  51.9 0.1 collective-permute-start.8
  52.0 0.7 dynamic_slice.3.scalars
  52.6 0.6 pad_add_fusion.1.which
  53.2 6.0 %collective-permute-done.8.other2 = bf16[640,128]{1,0:T(8,128)(2,1)S(1)} collective-permute-done((bf16[640,128]{1,0:T(8,128)(2,1)S(1)}, bf16[640,128]{1,0:T(8,128)(2,1)S(1)}, u32[]{:S(2)}, u32[]{:S(2)}) %collective-permute-start.8) | collective-permute-done | bytes 163872 | tf_op jit(solution)/shard_map/ppermute | solution.py:443
  59.2 0.0 collective-permute-done.4.other1
  59.2 0.6 copy-done.8
  59.8 0.7 copy-done.6
  60.5 13.7 %upper.1 = (bf16[256,512]{1,0:T(8,128)(2,1)}, bf16[512,512]{1,0:T(8,128)(2,1)}, bf16[2,720,128]{2,1,0:T(8,128)(2,1)}, bf16[2,640,128]{2,1,0:T(8,128)(2,1)}) custom-call(s32[3]{0:T(128)} %pad_add_fusion.1.which, f32[1]{0:T(128)} %dynamic_slice.3.scalars, bf16[720,128]{1,0:T(8,128)(2,1)} %copy-done, bf16[720,128]{1,0:T(8,128)(2,1)} %copy-done.6, ...), custom_call_target="tpu_custom_call" | custom-call | tf_op jit(solution)/shard_map/upper/pallas_call | solution.py:472
  74.2 1.1 select_bitcast_fusion.4
  75.3 0.1 collective-permute-start.9
  75.4 1.0 select_bitcast_fusion.6
  76.4 0.6 collective-permute-start.13
  77.0 0.1 collective-permute-start.17
  77.0 0.0 collective-permute-done.9
  77.0 1.1 bitcast_add_fusion
  78.1 1.9 %collective-permute-start.10 = (bf16[720,128]{1,0:T(8,128)(2,1)S(1)}, bf16[720,128]{1,0:T(8,128)(2,1)S(1)}, u32[]{:S(2)}, u32[]{:S(2)}) collective-permute-start(bf16[720,128]{1,0:T(8,128)(2,1)S(1)} %bitcast_add_fusion), channel_id=1, source_target_pairs={{0,8},{1,17},{2,10},{3,19},{4,12},{5,21},{6,14},{7,23},{8,0},{9,25... | collective-permute-start | bytes 552968 | tf_op jit(solution)/shard_map/ppermute | solution.py:516
  80.0 0.0 collective-permute-done.13
  80.0 1.0 bitcast_add_fusion.2
  81.0 0.2 collective-permute-start.14
  81.3 0.0 collective-permute-start.18
  81.3 0.6 pad_add_fusion.which
  81.9 4.6 %collective-permute-done.14 = bf16[640,128]{1,0:T(8,128)(2,1)S(1)} collective-permute-done((bf16[640,128]{1,0:T(8,128)(2,1)S(1)}, bf16[640,128]{1,0:T(8,128)(2,1)S(1)}, u32[]{:S(2)}, u32[]{:S(2)}) %collective-permute-start.14) | collective-permute-done | bytes 163872 | tf_op jit(solution)/shard_map/ppermute | solution.py:516
  86.5 0.4 collective-permute-start.15
  86.8 0.0 collective-permute-done.10
  86.8 0.1 add.61
  86.9 1.8 %collective-permute-start.11 = (bf16[720,128]{1,0:T(8,128)(2,1)S(1)}, bf16[720,128]{1,0:T(8,128)(2,1)S(1)}, u32[]{:S(2)}, u32[]{:S(2)}) collective-permute-start(bf16[720,128]{1,0:T(8,128)(2,1)S(1)} %add.61), channel_id=1, source_target_pairs={{0,16},{1,9},{2,18},{3,11},{4,20},{5,13},{6,22},{7,15},{8,24},{9,1... | collective-permute-start | bytes 552968 | tf_op jit(solution)/shard_map/ppermute | solution.py:516
  88.7 0.0 collective-permute-done.17
  88.7 0.7 select_bitcast_fusion.3
  89.4 0.8 pad_maximum_fusion.1
  90.3 1.6 %collective-permute-done.15 = bf16[640,128]{1,0:T(8,128)(2,1)S(1)} collective-permute-done((bf16[640,128]{1,0:T(8,128)(2,1)S(1)}, bf16[640,128]{1,0:T(8,128)(2,1)S(1)}, u32[]{:S(2)}, u32[]{:S(2)}) %collective-permute-start.15) | collective-permute-done | bytes 163872 | tf_op jit(solution)/shard_map/ppermute | solution.py:516
  91.9 0.1 collective-permute-start.16
  92.0 1.8 %collective-permute-done.11 = bf16[720,128]{1,0:T(8,128)(2,1)S(1)} collective-permute-done((bf16[720,128]{1,0:T(8,128)(2,1)S(1)}, bf16[720,128]{1,0:T(8,128)(2,1)S(1)}, u32[]{:S(2)}, u32[]{:S(2)}) %collective-permute-start.11) | collective-permute-done | bytes 184352 | tf_op jit(solution)/shard_map/ppermute | solution.py:516
  93.8 0.1 add.62.mine1
  93.9 0.1 collective-permute-start.12
  94.0 0.0 collective-permute-done.18
  94.0 0.1 select_bitcast_fusion.1
  94.1 1.3 %pad_maximum_fusion = bf16[2,512,512]{2,1,0:T(8,128)(2,1)} fusion(bf16[1,512,512]{2,1,0:T(8,128)(2,1)S(1)} %get-tuple-element.36, bf16[1,512,512]{2,1,0:T(8,128)(2,1)S(1)} %get-tuple-element.35), kind=kLoop, calls=%fused_computation | loop fusion | flops 524288 | bytes 2097152 | tf_op jit(solution)/shard_map/stack | solution.py:507
  95.4 0.0 collective-permute-done.16.other2
  95.4 0.0 collective-permute-done.12.other1
  95.4 0.7 copy-done.9
  96.1 0.0 copy-done.7
  96.1 19.6 %root.1 = (bf16[256,512]{1,0:T(8,128)(2,1)}, bf16[512,512]{1,0:T(8,128)(2,1)}, bf16[2,512,512]{2,1,0:T(8,128)(2,1)}, bf16[512,512]{1,0:T(8,128)(2,1)}, bf16[4,512,512]{2,1,0:T(8,128)(2,1)}) custom-call(s32[3]{0:T(128)} %pad_add_fusion.which, bf16[720,128]{1,0:T(8,128)(2,1)} %copy-done.1, bf16[720,128]{1,0:T(8,128)(2,1)} %copy-done.7, ...), custom_call_target="tpu_custom_call" | custom-call | tf_op jit(solution)/shard_map/root/pallas_call | solution.py:537
  (23 shorter events, 0.3 us)
Async XLA Ops:
  18.9 3.2 %collective-permute-start.5 = (bf16[2,640,128]{2,1,0:T(8,128)(2,1)}, bf16[2,640,128]{2,1,0:T(8,128)(2,1)S(1)}, u32[]{:S(2)}, u32[]{:S(2)}) collective-permute-start(bf16[2,640,128]{2,1,0:T(8,128)(2,1)} %get-tuple-element.23), channel_id=1, source_target_pairs={{0,1},{1,0},{2,3},{3,2},{4,5},{5,4},{6,7},{7,6},{8,9},{9,8},{10,11... | collective-permute-start | bytes 983048 | tf_op jit(solution)/shard_map/ppermute | solution.py:443
  19.4 3.8 %collective-permute-start.1 = (bf16[2,720,128]{2,1,0:T(8,128)(2,1)}, bf16[2,720,128]{2,1,0:T(8,128)(2,1)S(1)}, u32[]{:S(2)}, u32[]{:S(2)}) collective-permute-start(bf16[2,720,128]{2,1,0:T(8,128)(2,1)} %get-tuple-element.22), channel_id=1, source_target_pairs={{0,1},{1,0},{2,3},{3,2},{4,5},{5,4},{6,7},{7,6},{8,9},{9,8},{10,11... | collective-permute-start | bytes 1105928 | tf_op jit(solution)/shard_map/ppermute | solution.py:443
  20.1 1.3 %collective-permute-start = (f32[1,1]{1,0:T(1,128)}, f32[1,1]{1,0:T(1,128)}, u32[]{:S(2)}, u32[]{:S(2)}) collective-permute-start(f32[1,1]{1,0:T(1,128)} %bitcast.9), channel_id=1, source_target_pairs={{0,1},{1,0},{2,3},{3,2},{4,5},{5,4},{6,7},{7,6},{8,9},{9,8},{10,11... | collective-permute-start | bytes 20 | tf_op jit(solution)/shard_map/ppermute | solution.py:450
  23.2 28.8 %copy-start.10 = (f32[2]{0:T(128)S(1)}, f32[2]{0:T(128)}, u32[]{:S(2)}) copy-start(f32[2]{0:T(128)} %param.25) | copy-start | bytes 28
  24.4 6.4 %collective-permute-start.2 = (bf16[720,128]{1,0:T(8,128)(2,1)S(1)}, bf16[720,128]{1,0:T(8,128)(2,1)S(1)}, u32[]{:S(2)}, u32[]{:S(2)}) collective-permute-start(bf16[720,128]{1,0:T(8,128)(2,1)S(1)} %select_bitcast_fusion.5), channel_id=1, source_target_pairs={{0,2},{1,3},{2,0},{3,1},{4,6},{5,7},{6,4},{7,5},{8,10},{9,11},{10,... | collective-permute-start | bytes 552968 | tf_op jit(solution)/shard_map/ppermute | solution.py:443
  26.1 10.5 %collective-permute-start.6 = (bf16[640,128]{1,0:T(8,128)(2,1)S(1)}, bf16[640,128]{1,0:T(8,128)(2,1)S(1)}, u32[]{:S(2)}, u32[]{:S(2)}) collective-permute-start(bf16[640,128]{1,0:T(8,128)(2,1)S(1)} %select_bitcast_fusion.7), channel_id=1, source_target_pairs={{0,2},{1,3},{2,0},{3,1},{4,6},{5,7},{6,4},{7,5},{8,10},{9,11},{10,... | collective-permute-start | bytes 491528 | tf_op jit(solution)/shard_map/ppermute | solution.py:443
  30.8 18.8 %collective-permute-start.3 = (bf16[720,128]{1,0:T(8,128)(2,1)S(1)}, bf16[720,128]{1,0:T(8,128)(2,1)S(1)}, u32[]{:S(2)}, u32[]{:S(2)}) collective-permute-start(bf16[720,128]{1,0:T(8,128)(2,1)S(1)} %bitcast_add_fusion.1), channel_id=1, source_target_pairs={{0,4},{1,5},{2,6},{3,7},{4,0},{5,1},{6,2},{7,3},{8,12},{9,13},{10,... | collective-permute-start | bytes 552968 | tf_op jit(solution)/shard_map/ppermute | solution.py:443
  36.6 15.2 %collective-permute-start.7 = (bf16[640,128]{1,0:T(8,128)(2,1)S(1)}, bf16[640,128]{1,0:T(8,128)(2,1)S(1)}, u32[]{:S(2)}, u32[]{:S(2)}) collective-permute-start(bf16[640,128]{1,0:T(8,128)(2,1)S(1)} %bitcast_add_fusion.3), channel_id=1, source_target_pairs={{0,4},{1,5},{2,6},{3,7},{4,0},{5,1},{6,2},{7,3},{8,12},{9,13},{10,... | collective-permute-start | bytes 491528 | tf_op jit(solution)/shard_map/ppermute | solution.py:443
  49.6 9.6 %copy-start = (bf16[720,128]{1,0:T(8,128)(2,1)}, bf16[720,128]{1,0:T(8,128)(2,1)S(1)}, u32[]{:S(2)}) copy-start(bf16[720,128]{1,0:T(8,128)(2,1)S(1)} %add.56.mine1) | copy-start | bytes 552964
  49.6 9.6 %collective-permute-start.4 = (bf16[720,128]{1,0:T(8,128)(2,1)S(1)}, bf16[720,128]{1,0:T(8,128)(2,1)S(1)}, u32[]{:S(2)}, u32[]{:S(2)}) collective-permute-start(bf16[720,128]{1,0:T(8,128)(2,1)S(1)} %add.56.mine1), channel_id=1, source_target_pairs={{0,2},{1,3},{2,0},{3,1},{4,6},{5,7},{6,4},{7,5},{8,10},{9,11},{10,... | collective-permute-start | bytes 552968 | tf_op jit(solution)/shard_map/ppermute | solution.py:443
  51.9 7.3 %copy-start.2 = (bf16[640,128]{1,0:T(8,128)(2,1)}, bf16[640,128]{1,0:T(8,128)(2,1)S(1)}, u32[]{:S(2)}) copy-start(bf16[640,128]{1,0:T(8,128)(2,1)S(1)} %add.59.mine2) | copy-start | bytes 491524
  51.9 7.3 %collective-permute-start.8 = (bf16[640,128]{1,0:T(8,128)(2,1)S(1)}, bf16[640,128]{1,0:T(8,128)(2,1)S(1)}, u32[]{:S(2)}, u32[]{:S(2)}) collective-permute-start(bf16[640,128]{1,0:T(8,128)(2,1)S(1)} %add.59.mine2), channel_id=1, source_target_pairs={{0,2},{1,3},{2,0},{3,1},{4,6},{5,7},{6,4},{7,5},{8,10},{9,11},{10,... | collective-permute-start | bytes 491528 | tf_op jit(solution)/shard_map/ppermute | solution.py:443
  59.2 0.7 copy-start.8
  59.8 0.7 copy-start.6
  74.2 7.1 %copy-start.4 = (bf16[512,512]{1,0:T(8,128)(2,1)S(1)}, bf16[512,512]{1,0:T(8,128)(2,1)}, u32[]{:S(2)}) copy-start(bf16[512,512]{1,0:T(8,128)(2,1)} %get-tuple-element.30) | copy-start | bytes 1572868
  74.2 14.5 %copy-start.5 = (bf16[256,512]{1,0:T(8,128)(2,1)S(1)}, bf16[256,512]{1,0:T(8,128)(2,1)}, u32[]{:S(2)}) copy-start(bf16[256,512]{1,0:T(8,128)(2,1)} %get-tuple-element.26) | copy-start | bytes 786436
  75.3 1.7 %collective-permute-start.9 = (bf16[720,128]{1,0:T(8,128)(2,1)S(1)}, bf16[720,128]{1,0:T(8,128)(2,1)S(1)}, u32[]{:S(2)}, u32[]{:S(2)}) collective-permute-start(bf16[720,128]{1,0:T(8,128)(2,1)S(1)} %select_bitcast_fusion.4), channel_id=1, source_target_pairs={{0,1},{1,0},{2,3},{3,2},{4,5},{5,4},{6,7},{7,6},{8,9},{9,8},{10,11... | collective-permute-start | bytes 552968 | tf_op jit(solution)/shard_map/ppermute | solution.py:443
  76.4 3.6 %collective-permute-start.13 = (bf16[640,128]{1,0:T(8,128)(2,1)S(1)}, bf16[640,128]{1,0:T(8,128)(2,1)S(1)}, u32[]{:S(2)}, u32[]{:S(2)}) collective-permute-start(bf16[640,128]{1,0:T(8,128)(2,1)S(1)} %select_bitcast_fusion.6), channel_id=1, source_target_pairs={{0,1},{1,0},{2,3},{3,2},{4,5},{5,4},{6,7},{7,6},{8,9},{9,8},{10,11... | collective-permute-start | bytes 491528 | tf_op jit(solution)/shard_map/ppermute | solution.py:443
  77.0 11.7 %collective-permute-start.17 = (bf16[256,512]{1,0:T(8,128)(2,1)}, bf16[256,512]{1,0:T(8,128)(2,1)S(1)}, u32[]{:S(2)}, u32[]{:S(2)}) collective-permute-start(bf16[256,512]{1,0:T(8,128)(2,1)} %get-tuple-element.26), channel_id=1, source_target_pairs={{0,1},{1,0},{2,3},{3,2},{4,5},{5,4},{6,7},{7,6},{8,9},{9,8},{10,11... | collective-permute-start | bytes 786440 | tf_op jit(solution)/shard_map/ppermute | solution.py:443
  78.1 8.7 %collective-permute-start.10 = (bf16[720,128]{1,0:T(8,128)(2,1)S(1)}, bf16[720,128]{1,0:T(8,128)(2,1)S(1)}, u32[]{:S(2)}, u32[]{:S(2)}) collective-permute-start(bf16[720,128]{1,0:T(8,128)(2,1)S(1)} %bitcast_add_fusion), channel_id=1, source_target_pairs={{0,8},{1,17},{2,10},{3,19},{4,12},{5,21},{6,14},{7,23},{8,0},{9,25... | collective-permute-start | bytes 552968 | tf_op jit(solution)/shard_map/ppermute | solution.py:516
  81.0 5.4 %collective-permute-start.14 = (bf16[640,128]{1,0:T(8,128)(2,1)S(1)}, bf16[640,128]{1,0:T(8,128)(2,1)S(1)}, u32[]{:S(2)}, u32[]{:S(2)}) collective-permute-start(bf16[640,128]{1,0:T(8,128)(2,1)S(1)} %bitcast_add_fusion.2), channel_id=1, source_target_pairs={{0,8},{1,17},{2,10},{3,19},{4,12},{5,21},{6,14},{7,23},{8,0},{9,25... | collective-permute-start | bytes 491528 | tf_op jit(solution)/shard_map/ppermute | solution.py:516
  81.3 12.7 %collective-permute-start.18 = (bf16[512,512]{1,0:T(8,128)(2,1)S(1)}, bf16[512,512]{1,0:T(8,128)(2,1)S(1)}, u32[]{:S(2)}, u32[]{:S(2)}) collective-permute-start(bf16[512,512]{1,0:T(8,128)(2,1)S(1)} %copy-done.4), channel_id=1, source_target_pairs={{0,1},{1,0},{2,3},{3,2},{4,5},{5,4},{6,7},{7,6},{8,9},{9,8},{10,11... | collective-permute-start | bytes 1572872 | tf_op jit(solution)/shard_map/ppermute | solution.py:443
  86.5 5.4 %collective-permute-start.15 = (bf16[640,128]{1,0:T(8,128)(2,1)S(1)}, bf16[640,128]{1,0:T(8,128)(2,1)S(1)}, u32[]{:S(2)}, u32[]{:S(2)}) collective-permute-start(bf16[640,128]{1,0:T(8,128)(2,1)S(1)} %add.64), channel_id=1, source_target_pairs={{0,16},{1,9},{2,18},{3,11},{4,20},{5,13},{6,22},{7,15},{8,24},{9,1... | collective-permute-start | bytes 491528 | tf_op jit(solution)/shard_map/ppermute | solution.py:516
  86.9 6.9 %collective-permute-start.11 = (bf16[720,128]{1,0:T(8,128)(2,1)S(1)}, bf16[720,128]{1,0:T(8,128)(2,1)S(1)}, u32[]{:S(2)}, u32[]{:S(2)}) collective-permute-start(bf16[720,128]{1,0:T(8,128)(2,1)S(1)} %add.61), channel_id=1, source_target_pairs={{0,16},{1,9},{2,18},{3,11},{4,20},{5,13},{6,22},{7,15},{8,24},{9,1... | collective-permute-start | bytes 552968 | tf_op jit(solution)/shard_map/ppermute | solution.py:516
  91.9 3.4 %copy-start.3 = (bf16[640,128]{1,0:T(8,128)(2,1)}, bf16[640,128]{1,0:T(8,128)(2,1)S(1)}, u32[]{:S(2)}) copy-start(bf16[640,128]{1,0:T(8,128)(2,1)S(1)} %add.65.mine2) | copy-start | bytes 491524
  91.9 3.4 %collective-permute-start.16 = (bf16[640,128]{1,0:T(8,128)(2,1)S(1)}, bf16[640,128]{1,0:T(8,128)(2,1)S(1)}, u32[]{:S(2)}, u32[]{:S(2)}) collective-permute-start(bf16[640,128]{1,0:T(8,128)(2,1)S(1)} %add.65.mine2), channel_id=1, source_target_pairs={{0,1},{1,0},{2,3},{3,2},{4,5},{5,4},{6,7},{7,6},{8,9},{9,8},{10,11... | collective-permute-start | bytes 491528 | tf_op jit(solution)/shard_map/ppermute | solution.py:443
  93.9 1.5 %copy-start.1 = (bf16[720,128]{1,0:T(8,128)(2,1)}, bf16[720,128]{1,0:T(8,128)(2,1)S(1)}, u32[]{:S(2)}) copy-start(bf16[720,128]{1,0:T(8,128)(2,1)S(1)} %add.62.mine1) | copy-start | bytes 552964
  93.9 1.5 %collective-permute-start.12 = (bf16[720,128]{1,0:T(8,128)(2,1)S(1)}, bf16[720,128]{1,0:T(8,128)(2,1)S(1)}, u32[]{:S(2)}, u32[]{:S(2)}) collective-permute-start(bf16[720,128]{1,0:T(8,128)(2,1)S(1)} %add.62.mine1), channel_id=1, source_target_pairs={{0,1},{1,0},{2,3},{3,2},{4,5},{5,4},{6,7},{7,6},{8,9},{9,8},{10,11... | collective-permute-start | bytes 552968 | tf_op jit(solution)/shard_map/ppermute | solution.py:443
  95.4 0.7 copy-start.9
  95.4 0.7 copy-start.7
where the time goes:
time: 117 us; the launch traced here: 116 us
  Pallas kernels  48.9 us (42%)
  waiting for transfers between devices  29.8 us (25%)
  starting transfers between devices  18.6 us (16%)
  other arithmetic  10.9 us (9%)
  local copies, waits for them, and re-layouts  3.96 us (3%)
  between operations  3.45 us (3%)
    ppermute x14, waiting for transfers between devices, across(): return lax.ppermute(x, 'col', [(i, i ^ flip) for i in range(n_col)])  21.8 us
    pallas_call x1, Pallas kernels, local(): pl.pallas_call(root_kernel, out_shape=(matrix(NU, NX), matrix(NX, NX), ma...  19.6 us
    pallas_call x1, Pallas kernels, local(): pl.pallas_call(lower_kernel, grid=(slots,), out_shape=(matrix(NU, NX), ma...  15.7 us
    pallas_call x1, Pallas kernels, local(): pl.pallas_call(upper_kernel, out_shape=(matrix(NU, NX), matrix(NX, NX), m...  13.7 us
    ppermute x14, starting transfers between devices, across(): return lax.ppermute(x, 'col', [(i, i ^ flip) for i in range(n_col)])  13 us
    ppermute x4, waiting for transfers between devices, along(): lax.ppermute(x, ('row', 'col'), [(r * n_col + c, (r ^ 1 << bits[c % 2]) *...  7.97 us
    ppermute x4, starting transfers between devices, along(): lax.ppermute(x, ('row', 'col'), [(r * n_col + c, (r ^ 1 << bits[c % 2]) *...  4.31 us
  transfers between devices with their start and end apart: 19, of which 7 were waited for; matrix products, arithmetic and copies ran while one was open for 8% of the time, Pallas kernels for 0%

commit v1 on v0

v1 whole, which is shorter than its diff:
```python
import functools

import jax
import jax.numpy as jnp
from jax import lax
from jax.experimental import pallas as pl
from jax.experimental.pallas import tpu as pltpu
from jax.sharding import PartitionSpec as P

NX = 512
NU = 256
S1_ROW = 2
T = 128
HT = T // 2
WROWS = 16

f32 = jnp.float32
bf16 = jnp.bfloat16

FIRST = (
    ("bb", 0, 0), ("bb", 1, 0), ("bb", 1, 1), ("ba", 0, 0), ("ba", 0, 1), ("ba", 0, 2), ("ba", 0, 3),
)
SECOND = tuple(("ba", 1, j) for j in range(4)) + tuple(
    ("aa", i, j) for i in range(4) for j in range(i + 1)
)
PLACE = {name: (chunk, n) for chunk, names in enumerate((FIRST, SECOND)) for n, name in enumerate(names)}
ROWS = (len(FIRST) * HT + WROWS, len(SECOND) * HT + WROWS)

NN = (((1,), (0,)), ((), ()))
NT = (((1,), (1,)), ((), ()))
TN = (((0,), (0,)), ((), ()))


def dot(a, b, dims=NN):
    return lax.dot_general(a, b, dims, preferred_element_type=f32)


def split(x):
    high = x.astype(bf16)
    return high, (x - high.astype(f32)).astype(bf16)


def dot3(a, b, dims=NN):
    a_high, a_low = split(a)
    b_high, b_low = split(b)
    return dot(a_high, b_high, dims) + (dot(a_high, b_low, dims) + dot(a_low, b_high, dims))


def tree_sum(terms):
    while len(terms) > 1:
        terms = [terms[i] + terms[i + 1] for i in range(0, len(terms), 2)]
    return terms[0]


def row_of(x, k):
    return jnp.broadcast_to(x[k : k + 1, :], (8, T))


def column_of(x, k):
    return jnp.take_along_axis(x, jnp.full((8, T), k, jnp.int32), axis=1)


def parts_of(x):
    high = x.astype(bf16).astype(f32)
    rest = x - high
    middle = rest.astype(bf16).astype(f32)
    return high, middle, rest - middle


def negative_inverse(blocks):
    count = len(blocks)
    lane = lax.broadcasted_iota(jnp.int32, (8, T), 1)
    sub = lax.broadcasted_iota(jnp.int32, (8, T), 0)

    def pivot(block, first):
        cols = [column_of(block, first + k) for k in range(8)]
        for k in range(0, 8, 2):
            one, two = sub == k, sub == k + 1
            a = row_of(cols[k], k)
            b = row_of(cols[k + 1], k)
            c = row_of(cols[k + 1], k + 1)
            inverse = 1.0 / (a * c - b * b)
            left = jnp.where(one, -1.0, jnp.where(two, 0.0, cols[k]))
            right = jnp.where(two, -1.0, jnp.where(one, 0.0, cols[k + 1]))
            lead = (c * left - b * right) * inverse
            trail = (a * right - b * left) * inverse
            pair = one | two
            cols = [
                lead
                if j == k
                else trail
                if j == k + 1
                else (jnp.where(pair, 0.0, cols[j]) - lead * row_of(cols[j], k))
                - trail * row_of(cols[j], k + 1)
                for j in range(8)
            ]
        inside = (lane >= first) & (lane < first + 8)
        rows = jnp.where(inside, jnp.where(lane - first == sub, -1.0, 0.0), block)
        return tree_sum([cols[j] * row_of(rows, j) for j in range(8)])

    blocks = list(blocks)
    for i in range(count):
        first = 8 * i
        inside = (lane >= first) & (lane < first + 8)
        raw = blocks[i]
        lead = pivot(raw, first)
        near = [t for t in (i + 1,) if t < count]
        for t in near:
            added = tree_sum([column_of(blocks[t], first + k) * row_of(lead, k) for k in range(8)])
            blocks[t] = jnp.where(inside, 0.0, blocks[t]) + added
        h, m, l = parts_of(raw)
        a, b, c = parts_of(lead)
        far = dot(
            jnp.concatenate([h, h, m, m, h, l], axis=0).astype(bf16),
            jnp.concatenate([a, b, a, b, c, a], axis=0).astype(bf16),
            TN,
        )
        for t in range(count):
            if t != i and t not in near:
                blocks[t] = jnp.where(inside, 0.0, blocks[t]) + far[8 * t : 8 * t + 8, :]
        blocks[i] = -lead
    return blocks


def invert(source, target):
    rows = negative_inverse([source[8 * i : 8 * i + 8, :] for i in range(T // 8)])
    for i, row in enumerate(rows):
        target[8 * i : 8 * i + 8, :] = -row


def diagonal(block, costs_row):
    i = lax.broadcasted_iota(jnp.int32, block.shape, 0)
    j = lax.broadcasted_iota(jnp.int32, block.shape, 1)
    return block + jnp.where(i == j, jnp.broadcast_to(costs_row, block.shape), 0.0)


def eliminate(bb, control_cost, inv_a, through, schur):
    schur[...] = diagonal(bb(0, 0), control_cost[0:1, :])
    invert(schur, inv_a)
    h21 = bb(1, 0)
    through[...] = dot3(h21, inv_a[...])
    schur[...] = diagonal(bb(1, 1), control_cost[1:2, :]) - dot3(through[...], h21, NT)


def finish(block_ba, aa, inv_a, through, inv_s, state_cost, gain, value):
    top, bottom = block_ba[:T, :], block_ba[T:, :]
    below = dot3(inv_s[...], bottom - dot3(through[...], top))
    above = dot3(inv_a[...], top) - dot3(through[...], below, TN)
    feedback = -jnp.concatenate([above, below], axis=0)
    gain[...] = feedback.astype(bf16)
    for half in range(2):
        width = NU * (half + 1)
        rows = dot3(block_ba[:, NU * half : NU * half + NU], feedback[:, :width], TN)
        for bi in range(2):
            i = 2 * half + bi
            for j in range(i + 1):
                item = aa(i, j) + rows[T * bi : T * bi + T, T * j : T * j + T]
                if i == j:
                    item = diagonal(item, state_cost[i : i + 1, :])
                else:
                    value[T * j : T * j + T, T * i : T * i + T] = item.T.astype(bf16)
                value[T * i : T * i + T, T * j : T * j + T] = item.astype(bf16)


def lower_terms(states, inputs, applied):
    return (
        dot(inputs[...], applied[...], TN),
        dot(states[:, NU:], applied[:, :NX], TN),
        dot(states[:, :NU], applied[:, :NU], TN),
    )


def pack(parts, scale, weight_rows, outs):
    b_rows, a_high, a_low = parts
    for (kind, i, j), (chunk, n) in PLACE.items():
        if kind == "aa":
            source = a_low if i < 2 else a_high
            block = source[T * (i % 2) : T * (i % 2) + T, T * j : T * j + T]
        else:
            at = T * j + (NX if kind == "bb" else 0)
            block = b_rows[T * i : T * i + T, at : at + T]
        scaled = (scale * block).astype(bf16)
        for h in range(2):
            outs[chunk][h, HT * n : HT * n + HT, :] = scaled[HT * h : HT * h + HT, :]
    for h in range(2):
        for rows, out in zip(ROWS, outs):
            out[h, rows - WROWS :, :] = weight_rows


def spread_weight(weight, place, tag):
    lane = lax.broadcasted_iota(jnp.int32, (WROWS, T), 1)
    sub = lax.broadcasted_iota(jnp.int32, (WROWS, T), 0)
    full = jnp.full((WROWS, T), weight, f32)
    high = full.astype(bf16).astype(f32)
    item = jnp.where(sub == 0, high, jnp.where(sub == 1, full - high, 0.0))
    item = jnp.where(lane == place, item, 0.0)
    marks = jnp.full((WROWS, T), tag, jnp.int32).astype(f32)
    return jnp.where((sub == 2) & (lane == 0), marks, item).astype(bf16)


def sum_of_rows(rows, first, end):
    sub = lax.broadcasted_iota(jnp.int32, rows.shape, 0)
    return jnp.sum(jnp.where((sub >= first) & (sub < end), rows.astype(f32), 0.0))


def place_in_col():
    col = lax.axis_index("col")
    return col, lax.rem(col, 2), lax.rem(lax.div(col, 2), 2)


def local_sum_kernel(parent, mine, came, kept, sent):
    _, core, half = place_in_col()
    tag = sum_of_rows(came[0, mine.shape[1] - WROWS :, :], 2, 3)
    own = jnp.where(parent[0] == core, 1.0, 0.0)
    other = jnp.where(tag == core.astype(f32), 1.0, 0.0)
    for out, h in ((kept, half), (sent, 1 - half)):
        out[...] = (mine[h].astype(f32) * own + came[h].astype(f32) * other).astype(bf16)


def block_at(chunks, which, scale, name):
    chunk, n = PLACE[name]
    mine, other = chunks[2 * chunk], chunks[2 * chunk + 1]
    a = mine[HT * n : HT * n + HT, :].astype(f32) * scale
    b = other[HT * n : HT * n + HT, :].astype(f32) * scale
    swap = jnp.full((HT, T), which, jnp.int32) == 1
    return jnp.concatenate([jnp.where(swap, b, a), jnp.where(swap, a, b)], axis=0)


def solve_kernel(by_core, mine, other, control_cost, inv_a, through, inv_s, scale, schur):
    _, core, half = place_in_col()
    which = core if by_core else half
    weight = sum_of_rows(mine[ROWS[0] - WROWS :, :], 0, 2)
    scale[...] = 1.0 / jnp.full((HT, T), weight, f32)
    eliminate(
        lambda i, j: block_at((mine, other), which, scale[...], ("bb", i, j)),
        control_cost, inv_a, through, schur,
    )
    invert(schur, inv_s)


def finish_packed(which, chunks, solved, state_cost, gain, value):
    inv_a, through, inv_s, scale = solved

    def at(*name):
        return block_at(chunks, which, scale[...], name)

    block_ba = jnp.concatenate(
        [jnp.concatenate([at("ba", i, j) for j in range(4)], axis=1) for i in range(2)], axis=0
    )
    finish(
        block_ba, lambda i, j: at("aa", i, j), inv_a, through, inv_s, state_cost, gain, value
    )


def apply_value(value, states, inputs, applied):
    applied[:, :NX] = dot(value[...], states[...]).astype(bf16)
    applied[:, NX:] = dot(value[...], inputs[...]).astype(bf16)


def copies(pairs, sems):
    started = [
        pltpu.make_async_copy(source, target, sems.at[n]) for n, (source, target) in enumerate(pairs)
    ]
    for copy in started:
        copy.start()
    return started


def lower_kernel(
    count, mid_weight, parent, leaf_weight, leaf_state_hbm, leaf_input_hbm, mid_state_hbm,
    mid_input_hbm, state_cost, control_cost,
    gain, value, out1, out2,
    leaf_state, leaf_input, mid_state, mid_input, state_sems, input_sems, mid_sems,
    cost_cols, applied, acc_b, acc_high, acc_low, inv_a, through, schur, inv_s,
):
    slots = leaf_state.shape[0]
    live = count[0]
    for n in range(slots):
        pltpu.make_async_copy(leaf_state_hbm.at[n], leaf_state.at[n], state_sems.at[n]).start()
        pltpu.make_async_copy(leaf_input_hbm.at[n], leaf_input.at[n], input_sems.at[n]).start()
    mid_copies = copies(
        ((mid_state_hbm.at[0], mid_state), (mid_input_hbm.at[0], mid_input)), mid_sems
    )
    for i in range(NX // T):
        cost_cols[T * i : T * i + T, :] = jnp.broadcast_to(state_cost[i : i + 1, :], (T, T)).T
    acc_b[...] = jnp.zeros_like(acc_b)
    acc_high[...] = jnp.zeros_like(acc_high)
    acc_low[...] = jnp.zeros_like(acc_low)
    weights = leaf_weight[...].astype(f32)
    places = lax.broadcasted_iota(jnp.int32, weights.shape, 1)

    @pl.loop(0, slots)
    def _(slot):
        states, inputs = leaf_state.at[slot], leaf_input.at[slot]
        pltpu.make_async_copy(leaf_state_hbm.at[slot], states, state_sems.at[slot]).wait()
        pltpu.make_async_copy(leaf_input_hbm.at[slot], inputs, input_sems.at[slot]).wait()

        @pl.when(slot < live)
        def _():
            weight = jnp.sum(jnp.where(places == slot, weights, 0.0))
            cost = cost_cols[...]
            for j in range(NX // T):
                applied[:, T * j : T * j + T] = (
                    cost * states[:, T * j : T * j + T].astype(f32)
                ).astype(bf16)
            for j in range(NU // T):
                applied[:, NX + T * j : NX + T * j + T] = (
                    cost * inputs[:, T * j : T * j + T].astype(f32)
                ).astype(bf16)
            for acc, part in zip(
                (acc_b, acc_high, acc_low), lower_terms(states, inputs, applied)
            ):
                acc[...] += weight * part

    total = jnp.sum(jnp.where(places < live, weights, 0.0))
    mean_b = 1.0 / jnp.full((T, T), total, f32)
    scale = 1.0 / jnp.full((NU, NX), total, f32)
    eliminate(
        lambda i, j: acc_b[T * i : T * i + T, NX + T * j : NX + T * j + T] * mean_b,
        control_cost, inv_a, through, schur,
    )
    invert(schur, inv_s)
    finish(
        acc_b[:, :NX] * scale,
        lambda i, j: (acc_low if i < 2 else acc_high)[
            T * (i % 2) : T * (i % 2) + T, T * j : T * j + T
        ]
        * mean_b,
        inv_a, through, inv_s, state_cost, gain, value,
    )
    for copy in mid_copies:
        copy.wait()
    apply_value(value, mid_state, mid_input, applied)
    pack(
        lower_terms(mid_state, mid_input, applied),
        mid_weight[0],
        spread_weight(mid_weight[0], place_in_col()[0], parent[0]),
        (out1, out2),
    )


def close_kernel(leaf_state, leaf_input, gain, closed):
    closed[...] = (leaf_state[...].astype(f32) + dot(leaf_input[...], gain[...])).astype(bf16)


def upper_kernel(
    up_weight, mine1, other1, mine2, other2, inv_a, through, inv_s, scale,
    up_state_hbm, up_input_hbm, state_cost,
    gain, value, out1, out2,
    up_state, up_input, sems, applied,
):
    _, core, half = place_in_col()
    started = copies(
        ((up_state_hbm.at[core], up_state), (up_input_hbm.at[core], up_input)), sems
    )
    finish_packed(
        half, (mine1, other1, mine2, other2), (inv_a, through, inv_s, scale), state_cost, gain, value
    )
    for copy in started:
        copy.wait()
    apply_value(value, up_state, up_input, applied)
    weight = up_weight[core]
    pack(
        lower_terms(up_state, up_input, applied),
        weight,
        spread_weight(weight, lax.axis_index("row") * S1_ROW + core, core),
        (out1, out2),
    )


def spread(parent_cov, closed, noise_cov, moved, target):
    moved[...] = dot(closed[...], parent_cov[...]).astype(bf16)
    for i in range(NX // T):
        rows = dot(moved[T * i : T * i + T, :], closed[...], NT)
        for j in range(NX // T):
            item = rows[:, T * j : T * j + T]
            if i == j:
                item = diagonal(item, noise_cov[i : i + 1, :])
            target[T * i : T * i + T, T * j : T * j + T] = item.astype(bf16)


def root_kernel(
    count, parent, mine1, other1, mine2, other2, inv_a, through, inv_s, scale,
    state_cost, noise_cov, gain_own, gain_other, value_own, value_other, root_cov_hbm,
    up_state_hbm, up_input_hbm, mid_state_hbm, mid_input_hbm, closed_leaf_hbm,
    gain_out, value_out, up_gain, up_value, up_cov_out, mid_cov_out, leaf_cov_out,
    gain, value, root_cov, up_state, up_input, mid_state, mid_input, closed_leaf, parent_gain,
    up_cov, mid_cov, leaf_cov, closed, moved, in_sems, leaf_sems, out_sems, leaf_out_sems,
):
    _, core, _ = place_in_col()
    slots = closed_leaf.shape[0]
    live = count[0]
    arriving = copies(
        (
            (root_cov_hbm, root_cov),
            (up_state_hbm, up_state),
            (up_input_hbm, up_input),
            (mid_state_hbm.at[0], mid_state),
            (mid_input_hbm.at[0], mid_input),
        ),
        in_sems,
    )
    for n in range(slots):
        pltpu.make_async_copy(closed_leaf_hbm.at[n], closed_leaf.at[n], leaf_sems.at[n]).start()
    leaving = []

    def leave(source, target):
        copy = pltpu.make_async_copy(source, target, out_sems.at[len(leaving)])
        copy.start()
        leaving.append(copy)

    leave(gain_own, up_gain.at[core])
    leave(gain_other, up_gain.at[1 - core])
    leave(value_own, up_value.at[core])
    leave(value_other, up_value.at[1 - core])
    mine_is_parent = jnp.full((NU, NX), parent[0] - core, jnp.int32) == 0
    parent_gain[...] = jnp.where(
        mine_is_parent, gain_own[...].astype(f32), gain_other[...].astype(f32)
    ).astype(bf16)

    finish_packed(
        core, (mine1, other1, mine2, other2), (inv_a, through, inv_s, scale), state_cost, gain, value
    )
    leave(gain, gain_out)
    leave(value, value_out)
    for copy in arriving:
        copy.wait()
    for slot in range(S1_ROW):
        close_kernel(up_state.at[slot], up_input.at[slot], gain, closed)
        spread(root_cov, closed, noise_cov, moved, up_cov.at[slot])
    leave(up_cov, up_cov_out)
    close_kernel(mid_state, mid_input, parent_gain, closed)
    spread(up_cov.at[parent[0]], closed, noise_cov, moved, mid_cov)
    leave(mid_cov, mid_cov_out.at[0])

    @pl.loop(0, slots)
    def _(slot):
        pltpu.make_async_copy(
            closed_leaf_hbm.at[slot], closed_leaf.at[slot], leaf_sems.at[slot]
        ).wait()

        @pl.when(slot < live)
        def _():
            spread(mid_cov, closed_leaf.at[slot], noise_cov, moved, leaf_cov.at[slot])

        @pl.when(slot >= live)
        def _():
            leaf_cov[slot, :, :] = jnp.zeros((NX, NX), bf16)

        pltpu.make_async_copy(
            leaf_cov.at[slot], leaf_cov_out.at[slot], leaf_out_sems.at[slot]
        ).start()

    for copy in leaving:
        copy.wait()

    @pl.loop(0, slots)
    def _(slot):
        pltpu.make_async_copy(
            leaf_cov.at[slot], leaf_cov_out.at[slot], leaf_out_sems.at[slot]
        ).wait()


SMEM = pl.BlockSpec(memory_space=pltpu.SMEM)
VMEM = pl.BlockSpec(memory_space=pltpu.VMEM)
HBM = pl.BlockSpec(memory_space=pltpu.HBM)
DMA = pltpu.SemaphoreType.DMA


def limit(mib):
    return pltpu.CompilerParams(vmem_limit_bytes=mib << 20)


COST = pl.CostEstimate(flops=5 * 10**9, bytes_accessed=1 << 18, transcendentals=0)


def matrix(*shape, kind=bf16):
    return jax.ShapeDtypeStruct(shape, kind)


SQUARES = [pltpu.VMEM((T, T), f32)] * 4
PACKED = tuple(matrix(2, rows, T) for rows in ROWS)


def solve(by_core, chunk, control_rows):
    square = matrix(T, T, kind=f32)
    return pl.pallas_call(
        functools.partial(solve_kernel, by_core),
        out_shape=(square, square, square, matrix(HT, T, kind=f32)),
        in_specs=[VMEM] * 3,
        out_specs=(VMEM,) * 4,
        scratch_shapes=[pltpu.VMEM((T, T), f32)],
        compiler_params=limit(8),
        cost_estimate=COST,
        name="solve",
    )(*chunk, control_rows)


def local(
    n_row,
    n_col,
    leaf_state_map,
    leaf_input_map,
    leaf_weight,
    leaf_count,
    mid_state_map,
    mid_input_map,
    mid_weight,
    mid_parent,
    up_state_map,
    up_input_map,
    up_weight,
    root_cov,
    state_cost,
    control_cost,
    noise_cov,
):
    slots = leaf_state_map.shape[0]
    _, core, _ = place_in_col()
    state_rows = state_cost.reshape(NX // T, T)
    control_rows = control_cost.reshape(NU // T, T)
    noise_rows = noise_cov.reshape(NX // T, T)

    mid_gain, mid_value, *packed = pl.pallas_call(
        lower_kernel,
        out_shape=(matrix(NU, NX), matrix(NX, NX), *PACKED),
        in_specs=[SMEM] * 3 + [VMEM] + [HBM] * 4 + [VMEM] * 2,
        out_specs=(VMEM,) * 4,
        scratch_shapes=[
            pltpu.VMEM((slots, NX, NX), bf16),
            pltpu.VMEM((slots, NX, NU), bf16),
            pltpu.VMEM((NX, NX), bf16),
            pltpu.VMEM((NX, NU), bf16),
            DMA((slots,)),
            DMA((slots,)),
            DMA((2,)),
            pltpu.VMEM((NX, T), f32),
            pltpu.VMEM((NX, NX + NU), bf16),
            pltpu.VMEM((NU, NX + NU), f32),
            pltpu.VMEM((NU, NX), f32),
            pltpu.VMEM((NU, NU), f32),
            *SQUARES,
        ],
        compiler_params=pltpu.CompilerParams(vmem_limit_bytes=67043328),
        name="lower",
    )(
        leaf_count,
        mid_weight,
        mid_parent,
        leaf_weight.reshape(1, slots),
        leaf_state_map,
        leaf_input_map,
        mid_state_map,
        mid_input_map,
        state_rows,
        control_rows,
    )
    def across(x, flip):
        return lax.ppermute(x, "col", [(i, i ^ flip) for i in range(n_col)])

    def local_sum(x):
        part = matrix(*x.shape[1:])
        return pl.pallas_call(
            local_sum_kernel,
            out_shape=(part, part),
            in_specs=[SMEM, VMEM, VMEM],
            out_specs=(VMEM, VMEM),
            compiler_params=limit(8),
            name="local_sum",
        )(mid_parent, x, across(x, 1))

    def rest_of_col(kept):
        flip = 4
        while flip < n_col:
            kept = kept + across(kept, flip)
            flip = flip * 2
        return kept, across(kept, 2)

    (kept1, sent1), (kept2, sent2) = (local_sum(x) for x in packed)
    came1 = across(sent1, 2)
    came1, sent2 = lax.optimization_barrier((came1, sent2))
    came2 = across(sent2, 2)
    came2, gain_then = lax.optimization_barrier((came2, mid_gain))
    closed_leaf = pl.pallas_call(
        close_kernel,
        grid=(slots,),
        out_shape=matrix(slots, NX, NX),
        in_specs=[
            pl.BlockSpec((None, NX, NX), lambda n: (n, 0, 0)),
            pl.BlockSpec((None, NX, NU), lambda n: (n, 0, 0)),
            VMEM,
        ],
        out_specs=pl.BlockSpec((None, NX, NX), lambda n: (n, 0, 0)),
        compiler_params=limit(16),
        cost_estimate=pl.CostEstimate(
            flops=2 * slots * NX * NX * NU, bytes_accessed=slots * NX * 5 * NU * 2, transcendentals=0
        ),
        name="close",
    )(leaf_state_map, leaf_input_map, gain_then)
    first = rest_of_col(kept1 + came1)
    second = rest_of_col(kept2 + came2)
    solved = solve(False, first, control_rows)
    up_weight, closed_leaf = lax.optimization_barrier((up_weight, closed_leaf))

    up_gain_own, up_value_own, *packed = pl.pallas_call(
        upper_kernel,
        out_shape=(matrix(NU, NX), matrix(NX, NX), *PACKED),
        in_specs=[SMEM] + [VMEM] * 8 + [HBM] * 2 + [VMEM],
        out_specs=(VMEM,) * 4,
        scratch_shapes=[
            pltpu.VMEM((NX, NX), bf16),
            pltpu.VMEM((NX, NU), bf16),
            DMA((2,)),
            pltpu.VMEM((NX, NX + NU), bf16),
        ],
        compiler_params=limit(24),
        name="upper",
    )(up_weight, *first, *second, *solved, up_state_map, up_input_map, state_rows)
    up_gain_other = across(up_gain_own, 1)
    up_value_other = across(up_value_own, 1)

    row_bits = n_row.bit_length() - 1
    is_low = core == 0

    def along(x, step):
        bits = (step % row_bits, (step + row_bits // 2) % row_bits)
        return lax.ppermute(
            x,
            ("row", "col"),
            [
                (r * n_col + c, (r ^ (1 << bits[c % 2])) * n_col + c)
                for r in range(n_row)
                for c in range(n_col)
            ],
        )

    def chip_sum(x):
        sent = jnp.where(is_low, x[1], x[0])
        return jnp.where(is_low, x[0], x[1]) + across(sent, 1)

    def rest_of_row(kept):
        for step in range(1, row_bits):
            kept = kept + along(kept, step)
        return kept, across(kept, 1)

    kept1, kept2 = (chip_sum(x) for x in packed)
    came1 = along(kept1, 0)
    came1, kept2 = lax.optimization_barrier((came1, kept2))
    came2 = along(kept2, 0)
    first = rest_of_row(kept1 + came1)
    second = rest_of_row(kept2 + came2)
    solved = solve(True, first, control_rows)

    root_gain, root_value, up_gain, up_value, up_cov, mid_cov, leaf_cov = pl.pallas_call(
        root_kernel,
        out_shape=(
            matrix(NU, NX),
            matrix(NX, NX),
            matrix(S1_ROW, NU, NX),
            matrix(S1_ROW, NX, NX),
            matrix(S1_ROW, NX, NX),
            matrix(1, NX, NX),
            matrix(slots, NX, NX),
        ),
        in_specs=[SMEM] * 2 + [VMEM] * 14 + [HBM] * 6,
        out_specs=(HBM,) * 7,
        scratch_shapes=[
            pltpu.VMEM((NU, NX), bf16),
            pltpu.VMEM((NX, NX), bf16),
            pltpu.VMEM((NX, NX), bf16),
            pltpu.VMEM((S1_ROW, NX, NX), bf16),
            pltpu.VMEM((S1_ROW, NX, NU), bf16),
            pltpu.VMEM((NX, NX), bf16),
            pltpu.VMEM((NX, NU), bf16),
            pltpu.VMEM((slots, NX, NX), bf16),
            pltpu.VMEM((NU, NX), bf16),
            pltpu.VMEM((S1_ROW, NX, NX), bf16),
            pltpu.VMEM((NX, NX), bf16),
            pltpu.VMEM((slots, NX, NX), bf16),
            pltpu.VMEM((NX, NX), bf16),
            pltpu.VMEM((NX, NX), bf16),
            DMA((5,)),
            DMA((slots,)),
            DMA((8,)),
            DMA((slots,)),
        ],
        compiler_params=limit(32),
        name="root",
    )(
        leaf_count,
        mid_parent,
        *first,
        *second,
        *solved,
        state_rows,
        noise_rows,
        up_gain_own,
        up_gain_other,
        up_value_own,
        up_value_other,
        root_cov,
        up_state_map,
        up_input_map,
        mid_state_map,
        mid_input_map,
        closed_leaf,
    )
    return (
        root_gain,
        root_value,
        up_gain,
        up_value,
        up_cov,
        mid_gain[None],
        mid_value[None],
        mid_cov,
        leaf_cov,
    )


def solution(mesh):
    both = P(("row", "col"), None, None)
    flat = P(("row", "col"))
    up = P("row", None, None)
    return jax.shard_map(
        functools.partial(local, mesh.shape["row"], mesh.shape["col"]),
        mesh=mesh,
        in_specs=(
            both, both, flat, flat, both, both, flat, flat, up, up, P("row"), P(), P(), P(), P(),
        ),
        out_specs=(P(), P(), up, up, up, both, both, both, both),
        check_vma=False,
    )
```

time: 117 us -> 96.7 us (0.83); the launches traced: 116 us -> 96.6 us
  other arithmetic: 10.9 us -> 0.51 us
  Pallas kernels: 48.9 us -> 42.1 us
  starting transfers between devices: 18.6 us -> 15.6 us
  waiting for transfers between devices: 29.8 us -> 32.1 us
    pallas_call x1, Pallas kernels: 19.6 us -> 10.3 us  [local(): pl.pallas_call(root_kernel, out_shape=(matrix(NU, NX), matrix(NX, NX), ma...]
    ppermute x4, waiting for transfers between devices: 7.97 us -> 13.3 us  [along(): lax.ppermute(x, ('row', 'col'), [(r * n_col + c, (r ^ 1 << bits[c % 2]) *...]
    another operation x6 -> x0, other arithmetic: 4.08 us -> none  [the longest x2 1.59 us: local(): jnp.stack([select(is_low, up_gain_own, up_gain_other), select(is_low, up_...]
    ppermute x14, waiting for transfers between devices: 21.8 us -> 18.8 us  [across(): return lax.ppermute(x, 'col', [(i, i ^ flip) for i in range(n_col)])]
    pallas_call x2 -> x7, Pallas kernels: 29.3 us -> 31.8 us  [the longest x1 14.1 us: local(): pl.pallas_call(lower_kernel, out_shape=(matrix(NU, NX), matrix(NX, NX), *...]
    convert_element_type x2 -> x0, other arithmetic: 2.26 us -> none  [reduce_col(): both = both.astype(bf16)]
    select_n x4 -> x2, other arithmetic: 2.16 us -> 0.04 us  [chip_sum(): sent = jnp.where(is_low, x[1], x[0])]
    add x10, other arithmetic: 2.44 us -> 0.47 us  [the longest x2 0.1 us: rest_of_row(): kept = kept + along(kept, step)]
  transfers between devices with their start and end apart: 19 -> 18, of which waited for: 7 -> 9; matrix products, arithmetic and copies ran while one was open for 8% -> 1% of each run, Pallas kernels for 0% -> 15%
where the time goes in v1:
time: 96.7 us; the launch traced here: 96.6 us
  Pallas kernels  42.1 us (44%)
  waiting for transfers between devices  32.1 us (33%)
  starting transfers between devices  15.6 us (16%)
  local copies, waits for them, and re-layouts  3.25 us (3%)
  between operations  3.06 us (3%)
    ppermute x14, waiting for transfers between devices, across(): return lax.ppermute(x, 'col', [(i, i ^ flip) for i in range(n_col)])  18.8 us
    pallas_call x1, Pallas kernels, local(): pl.pallas_call(lower_kernel, out_shape=(matrix(NU, NX), matrix(NX, NX), *...  14.1 us
    ppermute x4, waiting for transfers between devices, along(): lax.ppermute(x, ('row', 'col'), [(r * n_col + c, (r ^ 1 << bits[c % 2]) *...  13.3 us
    pallas_call x2, Pallas kernels, solve(): pl.pallas_call(functools.partial(solve_kernel, by_core), out_shape=(squar...  12.7 us
    ppermute x14, starting transfers between devices, across(): return lax.ppermute(x, 'col', [(i, i ^ flip) for i in range(n_col)])  11.4 us
    pallas_call x1, Pallas kernels, local(): pl.pallas_call(root_kernel, out_shape=(matrix(NU, NX), matrix(NX, NX), ma...  10.3 us
    ppermute x4, starting transfers between devices, along(): lax.ppermute(x, ('row', 'col'), [(r * n_col + c, (r ^ 1 << bits[c % 2]) *...  4.23 us
    pallas_call x1, Pallas kernels, local(): pl.pallas_call(upper_kernel, out_shape=(matrix(NU, NX), matrix(NX, NX), *...  3.26 us
  transfers between devices with their start and end apart: 18, of which 9 were waited for; matrix products, arithmetic and copies ran while one was open for 1% of the time, Pallas kernels for 15%

profile of v1, /device:TPU:0, one launch (start us, length us, event | category | flops | bytes accessed | tf_op | source)
XLA Modules:
  0.0 96.6 jit_solution(13332849690483602965)
XLA Ops:
  2.6 14.1 %lower.1 = (bf16[256,512]{1,0:T(8,128)(2,1)}, bf16[512,512]{1,0:T(8,128)(2,1)}, bf16[2,464,128]{2,1,0:T(8,128)(2,1)}, bf16[2,912,128]{2,1,0:T(8,128)(2,1)}) custom-call(s32[1]{0:T(128)S(6)} %copy.24.count, f32[1]{0:T(128)S(6)} %copy.25.mid_weight, s32[1]{0:T(128)S(6)} %copy.26.parent, bf16[1,4]{1,0:T(2,128)(2,1)} %bitcast.22, ...), custom_call_target="tpu_custom_call" | custom-call | tf_op jit(solution)/shard_map/lower/pallas_call | solution.py:524
  16.7 0.0 copy-start
  16.7 0.1 collective-permute-start.2
  16.8 0.5 collective-permute-start
  17.3 1.9 %collective-permute-done.came = bf16[2,464,128]{2,1,0:T(8,128)(2,1)S(1)} collective-permute-done((bf16[2,464,128]{2,1,0:T(8,128)(2,1)}, bf16[2,464,128]{2,1,0:T(8,128)(2,1)S(1)}, u32[]{:S(2)}, u32[]{:S(2)}) %collective-permute-start) | collective-permute-done | bytes 237600 | tf_op jit(solution)/shard_map/ppermute | solution.py:559
  19.2 0.9 copy-done.9
  20.1 0.2 local_sum.2
  20.3 3.1 %collective-permute-start.1 = (bf16[464,128]{1,0:T(8,128)(2,1)S(1)}, bf16[464,128]{1,0:T(8,128)(2,1)S(1)}, u32[]{:S(2)}, u32[]{:S(2)}) collective-permute-start(bf16[464,128]{1,0:T(8,128)(2,1)S(1)} %get-tuple-element.45), channel_id=1, source_target_pairs={{0,2},{1,3},{2,0},{3,1},{4,6},{5,7},{6,4},{7,5},{8,10},{9,11},{10,... | collective-permute-start | bytes 356360 | tf_op jit(solution)/shard_map/ppermute | solution.py:559
  23.4 0.0 collective-permute-done.2.came
  23.4 1.0 %copy-done.7 = bf16[2,912,128]{2,1,0:T(8,128)(2,1)S(1)} copy-done((bf16[2,912,128]{2,1,0:T(8,128)(2,1)S(1)}, bf16[2,912,128]{2,1,0:T(8,128)(2,1)}, u32[]{:S(2)}) %copy-start.7) | copy-done | bytes 466968
  24.4 0.3 local_sum.3
  24.8 2.2 %collective-permute-done.1 = bf16[464,128]{1,0:T(8,128)(2,1)S(1)} collective-permute-done((bf16[464,128]{1,0:T(8,128)(2,1)S(1)}, bf16[464,128]{1,0:T(8,128)(2,1)S(1)}, u32[]{:S(2)}, u32[]{:S(2)}) %collective-permute-start.1) | collective-permute-done | bytes 118816 | tf_op jit(solution)/shard_map/ppermute | solution.py:559
  27.0 1.7 %collective-permute-start.3 = (bf16[912,128]{1,0:T(8,128)(2,1)S(1)}, bf16[912,128]{1,0:T(8,128)(2,1)S(1)}, u32[]{:S(2)}, u32[]{:S(2)}) collective-permute-start(bf16[912,128]{1,0:T(8,128)(2,1)S(1)} %get-tuple-element.48), channel_id=1, source_target_pairs={{0,2},{1,3},{2,0},{3,1},{4,6},{5,7},{6,4},{7,5},{8,10},{9,11},{10,... | collective-permute-start | bytes 700424 | tf_op jit(solution)/shard_map/ppermute | solution.py:559
  28.7 1.4 %collective-permute-start.4 = (bf16[464,128]{1,0:T(8,128)(2,1)S(1)}, bf16[464,128]{1,0:T(8,128)(2,1)S(1)}, u32[]{:S(2)}, u32[]{:S(2)}) collective-permute-start(bf16[464,128]{1,0:T(8,128)(2,1)S(1)} %add.30), channel_id=1, source_target_pairs={{0,4},{1,5},{2,6},{3,7},{4,0},{5,1},{6,2},{7,3},{8,12},{9,13},{10,... | collective-permute-start | bytes 356360 | tf_op jit(solution)/shard_map/ppermute | solution.py:559
  30.1 6.6 %collective-permute-done.3 = bf16[912,128]{1,0:T(8,128)(2,1)S(1)} collective-permute-done((bf16[912,128]{1,0:T(8,128)(2,1)S(1)}, bf16[912,128]{1,0:T(8,128)(2,1)S(1)}, u32[]{:S(2)}, u32[]{:S(2)}) %collective-permute-start.3) | collective-permute-done | bytes 233504 | tf_op jit(solution)/shard_map/ppermute | solution.py:559
  36.7 0.1 add.32
  36.7 1.3 %collective-permute-start.6 = (bf16[912,128]{1,0:T(8,128)(2,1)S(1)}, bf16[912,128]{1,0:T(8,128)(2,1)S(1)}, u32[]{:S(2)}, u32[]{:S(2)}) collective-permute-start(bf16[912,128]{1,0:T(8,128)(2,1)S(1)} %add.32), channel_id=1, source_target_pairs={{0,4},{1,5},{2,6},{3,7},{4,0},{5,1},{6,2},{7,3},{8,12},{9,13},{10,... | collective-permute-start | bytes 700424 | tf_op jit(solution)/shard_map/ppermute | solution.py:559
  38.0 0.0 collective-permute-done.4
  38.0 1.9 %collective-permute-start.5 = (bf16[464,128]{1,0:T(8,128)(2,1)S(1)}, bf16[464,128]{1,0:T(8,128)(2,1)S(1)}, u32[]{:S(2)}, u32[]{:S(2)}) collective-permute-start(bf16[464,128]{1,0:T(8,128)(2,1)S(1)} %add.31.mine.mine1), channel_id=1, source_target_pairs={{0,2},{1,3},{2,0},{3,1},{4,6},{5,7},{6,4},{7,5},{8,10},{9,11},{10,... | collective-permute-start | bytes 356360 | tf_op jit(solution)/shard_map/ppermute | solution.py:559
  39.9 1.2 %copy-done.2 = bf16[4,512,256]{2,1,0:T(8,128)(2,1)S(1)} copy-done((bf16[4,512,256]{2,1,0:T(8,128)(2,1)S(1)}, bf16[4,512,256]{2,1,0:T(8,128)(2,1)}, u32[]{:S(2)}) %copy-start.2) | copy-done | bytes 1048600
  41.2 1.2 %close.1.closed_leaf_hbm = bf16[4,512,512]{2,1,0:T(8,128)(2,1)S(1)} custom-call(bf16[4,512,512]{2,1,0:T(8,128)(2,1)S(1)} %copy-done, bf16[4,512,256]{2,1,0:T(8,128)(2,1)S(1)} %copy-done.2, bf16[256,512]{1,0:T(8,128)(2,1)S(1)} %copy-done.8), custom_call_target="tpu_custom_call" | custom-call | flops 536870912 | bytes 5242880 | tf_op jit(solution)/shard_map/close/pallas_call | solution.py:584
  42.4 6.2 %collective-permute-done.6 = bf16[912,128]{1,0:T(8,128)(2,1)S(1)} collective-permute-done((bf16[912,128]{1,0:T(8,128)(2,1)S(1)}, bf16[912,128]{1,0:T(8,128)(2,1)S(1)}, u32[]{:S(2)}, u32[]{:S(2)}) %collective-permute-start.6) | collective-permute-done | bytes 233504 | tf_op jit(solution)/shard_map/ppermute | solution.py:559
  48.6 0.1 add.33.mine2
  48.6 0.0 copy-start.1
  48.7 0.0 copy-start.4
  48.7 0.0 copy-start.10
  48.7 0.0 copy-start.13
  48.7 0.1 collective-permute-start.7
  48.8 0.0 collective-permute-done.5.other.other1
  48.8 0.0 copy-done.12
  48.8 6.4 %solve.2 = (f32[128,128]{1,0:T(8,128)S(1)}, f32[128,128]{1,0:T(8,128)S(1)}, f32[128,128]{1,0:T(8,128)S(1)}, f32[64,128]{1,0:T(8,128)S(1)}) custom-call(bf16[464,128]{1,0:T(8,128)(2,1)S(1)} %add.31.mine.mine1, bf16[464,128]{1,0:T(8,128)(2,1)S(1)} %collective-permute-done.5.other.other1, f32[2,128]{1,0:T(2,128)S(1)} %bitcast.20), custom_call_target="tpu_custom_call" | custom-call | flops 5000000000 | bytes 262144 | tf_op jit(solution)/shard_map/solve/pallas_call | solution.py:487
  55.2 1.2 %collective-permute-done.7.other2 = bf16[912,128]{1,0:T(8,128)(2,1)S(1)} collective-permute-done((bf16[912,128]{1,0:T(8,128)(2,1)S(1)}, bf16[912,128]{1,0:T(8,128)(2,1)S(1)}, u32[]{:S(2)}, u32[]{:S(2)}) %collective-permute-start.7) | collective-permute-done | bytes 233504 | tf_op jit(solution)/shard_map/ppermute | solution.py:559
  56.4 0.0 copy-done.13
  56.4 3.3 %upper.1 = (bf16[256,512]{1,0:T(8,128)(2,1)S(1)}, bf16[512,512]{1,0:T(8,128)(2,1)S(1)}, bf16[2,464,128]{2,1,0:T(8,128)(2,1)S(1)}, bf16[2,912,128]{2,1,0:T(8,128)(2,1)S(1)}) custom-call(f32[2]{0:T(128)S(1)} %copy-done.13, bf16[464,128]{1,0:T(8,128)(2,1)S(1)} %add.31.mine.mine1, bf16[464,128]{1,0:T(8,128)(2,1)S(1)} %collective-permute-done.5.other.other1, ...), custom_call_target="tpu_custom_call" | custom-call | tf_op jit(solution)/shard_map/upper/pallas_call | solution.py:605
  59.7 0.1 collective-permute-start.8
  59.8 0.6 collective-permute-start.10
  60.4 0.7 collective-permute-done.8
  61.1 1.1 %collective-permute-start.9 = (bf16[464,128]{1,0:T(8,128)(2,1)S(1)}, bf16[464,128]{1,0:T(8,128)(2,1)S(1)}, u32[]{:S(2)}, u32[]{:S(2)}) collective-permute-start(bf16[464,128]{1,0:T(8,128)(2,1)S(1)} %bitcast_add_fusion.1), channel_id=1, source_target_pairs={{0,8},{1,17},{2,10},{3,19},{4,12},{5,21},{6,14},{7,23},{8,0},{9,25... | collective-permute-start | bytes 356360 | tf_op jit(solution)/shard_map/ppermute | solution.py:627
  62.2 0.0 collective-permute-done.10
  62.2 0.1 bitcast_add_fusion
  62.2 3.8 %collective-permute-done.9 = bf16[464,128]{1,0:T(8,128)(2,1)S(1)} collective-permute-done((bf16[464,128]{1,0:T(8,128)(2,1)S(1)}, bf16[464,128]{1,0:T(8,128)(2,1)S(1)}, u32[]{:S(2)}, u32[]{:S(2)}) %collective-permute-start.9) | collective-permute-done | bytes 118816 | tf_op jit(solution)/shard_map/ppermute | solution.py:627
  66.0 1.0 %collective-permute-start.13 = (bf16[912,128]{1,0:T(8,128)(2,1)S(1)}, bf16[912,128]{1,0:T(8,128)(2,1)S(1)}, u32[]{:S(2)}, u32[]{:S(2)}) collective-permute-start(bf16[912,128]{1,0:T(8,128)(2,1)S(1)} %bitcast_add_fusion), channel_id=1, source_target_pairs={{0,8},{1,17},{2,10},{3,19},{4,12},{5,21},{6,14},{7,23},{8,0},{9,25... | collective-permute-start | bytes 700424 | tf_op jit(solution)/shard_map/ppermute | solution.py:627
  67.0 1.4 %collective-permute-start.11 = (bf16[464,128]{1,0:T(8,128)(2,1)S(1)}, bf16[464,128]{1,0:T(8,128)(2,1)S(1)}, u32[]{:S(2)}, u32[]{:S(2)}) collective-permute-start(bf16[464,128]{1,0:T(8,128)(2,1)S(1)} %add.36), channel_id=1, source_target_pairs={{0,16},{1,9},{2,18},{3,11},{4,20},{5,13},{6,22},{7,15},{8,24},{9,1... | collective-permute-start | bytes 356360 | tf_op jit(solution)/shard_map/ppermute | solution.py:627
  68.4 4.9 %collective-permute-done.13 = bf16[912,128]{1,0:T(8,128)(2,1)S(1)} collective-permute-done((bf16[912,128]{1,0:T(8,128)(2,1)S(1)}, bf16[912,128]{1,0:T(8,128)(2,1)S(1)}, u32[]{:S(2)}, u32[]{:S(2)}) %collective-permute-start.13) | collective-permute-done | bytes 233504 | tf_op jit(solution)/shard_map/ppermute | solution.py:627
  73.3 0.1 add.38
  73.4 0.8 collective-permute-start.14
  74.2 0.0 collective-permute-done.11
  74.2 0.1 collective-permute-start.12
  74.3 0.5 collective-permute-start.17
  74.8 0.1 collective-permute-start.16
  74.9 4.7 %collective-permute-done.14 = bf16[912,128]{1,0:T(8,128)(2,1)S(1)} collective-permute-done((bf16[912,128]{1,0:T(8,128)(2,1)S(1)}, bf16[912,128]{1,0:T(8,128)(2,1)S(1)}, u32[]{:S(2)}, u32[]{:S(2)}) %collective-permute-start.14) | collective-permute-done | bytes 233504 | tf_op jit(solution)/shard_map/ppermute | solution.py:627
  79.5 0.1 add.39.mine2
  79.6 0.0 copy-start.3
  79.6 0.0 copy-start.5
  79.6 0.0 copy-start.6
  79.6 0.0 copy-start.11
  79.7 0.1 collective-permute-start.15
  79.7 0.0 collective-permute-done.12.other.other1
  79.7 6.4 %solve.3 = (f32[128,128]{1,0:T(8,128)S(1)}, f32[128,128]{1,0:T(8,128)S(1)}, f32[128,128]{1,0:T(8,128)S(1)}, f32[64,128]{1,0:T(8,128)S(1)}) custom-call(bf16[464,128]{1,0:T(8,128)(2,1)S(1)} %add.37.mine.mine1, bf16[464,128]{1,0:T(8,128)(2,1)S(1)} %collective-permute-done.12.other.other1, f32[2,128]{1,0:T(2,128)S(1)} %bitcast.21), custom_call_target="tpu_custom_call" | custom-call | flops 5000000000 | bytes 262144 | tf_op jit(solution)/shard_map/solve/pallas_call | solution.py:487
  86.1 0.0 collective-permute-done.16.gain_other
  86.1 0.0 collective-permute-done.17.value_other
  86.1 0.0 collective-permute-done.15.other2
  86.2 0.0 copy-done.3
  86.2 10.3 %root.1 = (bf16[256,512]{1,0:T(8,128)(2,1)}, bf16[512,512]{1,0:T(8,128)(2,1)}, bf16[2,256,512]{2,1,0:T(8,128)(2,1)}, bf16[2,512,512]{2,1,0:T(8,128)(2,1)}, bf16[...) custom-call(s32[1]{0:T(128)S(6)} %copy.24.count, s32[1]{0:T(128)S(6)} %copy.26.parent, ...), custom_call_target="tpu_custom_call" | custom-call | tf_op jit(solution)/shard_map/root/pallas_call | solution.py:654
  (20 shorter events, 0.2 us)
Async XLA Ops:
  16.7 23.2 %copy-start = (bf16[4,512,512]{2,1,0:T(8,128)(2,1)S(1)}, bf16[4,512,512]{2,1,0:T(8,128)(2,1)}, u32[]{:S(2)}) copy-start(bf16[4,512,512]{2,1,0:T(8,128)(2,1)} %leaf_state.1) | copy-start | bytes 6291460
  16.7 6.7 %collective-permute-start.2 = (bf16[2,912,128]{2,1,0:T(8,128)(2,1)}, bf16[2,912,128]{2,1,0:T(8,128)(2,1)S(1)}, u32[]{:S(2)}, u32[]{:S(2)}) collective-permute-start(bf16[2,912,128]{2,1,0:T(8,128)(2,1)} %get-tuple-element.46.mine), channel_id=1, source_target_pairs={{0,1},{1,0},{2,3},{3,2},{4,5},{5,4},{6,7},{7,6},{8,9},{9,8},{10,11... | collective-permute-start | bytes 1400840 | tf_op jit(solution)/shard_map/ppermute | solution.py:559
  16.8 2.4 %collective-permute-start = (bf16[2,464,128]{2,1,0:T(8,128)(2,1)}, bf16[2,464,128]{2,1,0:T(8,128)(2,1)S(1)}, u32[]{:S(2)}, u32[]{:S(2)}) collective-permute-start(bf16[2,464,128]{2,1,0:T(8,128)(2,1)} %get-tuple-element.44.mine), channel_id=1, source_target_pairs={{0,1},{1,0},{2,3},{3,2},{4,5},{5,4},{6,7},{7,6},{8,9},{9,8},{10,11... | collective-permute-start | bytes 712712 | tf_op jit(solution)/shard_map/ppermute | solution.py:559
  19.2 0.9 copy-start.9
  20.3 6.7 %collective-permute-start.1 = (bf16[464,128]{1,0:T(8,128)(2,1)S(1)}, bf16[464,128]{1,0:T(8,128)(2,1)S(1)}, u32[]{:S(2)}, u32[]{:S(2)}) collective-permute-start(bf16[464,128]{1,0:T(8,128)(2,1)S(1)} %get-tuple-element.45), channel_id=1, source_target_pairs={{0,2},{1,3},{2,0},{3,1},{4,6},{5,7},{6,4},{7,5},{8,10},{9,11},{10,... | collective-permute-start | bytes 356360 | tf_op jit(solution)/shard_map/ppermute | solution.py:559
  23.4 1.0 %copy-start.7 = (bf16[2,912,128]{2,1,0:T(8,128)(2,1)S(1)}, bf16[2,912,128]{2,1,0:T(8,128)(2,1)}, u32[]{:S(2)}) copy-start(bf16[2,912,128]{2,1,0:T(8,128)(2,1)} %get-tuple-element.46.mine) | copy-start | bytes 1400836
  24.4 15.5 %copy-start.8 = (bf16[256,512]{1,0:T(8,128)(2,1)S(1)}, bf16[256,512]{1,0:T(8,128)(2,1)}, u32[]{:S(2)}) copy-start(bf16[256,512]{1,0:T(8,128)(2,1)} %get-tuple-element.50.gain) | copy-start | bytes 786436
  27.0 9.7 %collective-permute-start.3 = (bf16[912,128]{1,0:T(8,128)(2,1)S(1)}, bf16[912,128]{1,0:T(8,128)(2,1)S(1)}, u32[]{:S(2)}, u32[]{:S(2)}) collective-permute-start(bf16[912,128]{1,0:T(8,128)(2,1)S(1)} %get-tuple-element.48), channel_id=1, source_target_pairs={{0,2},{1,3},{2,0},{3,1},{4,6},{5,7},{6,4},{7,5},{8,10},{9,11},{10,... | collective-permute-start | bytes 700424 | tf_op jit(solution)/shard_map/ppermute | solution.py:559
  28.7 9.3 %collective-permute-start.4 = (bf16[464,128]{1,0:T(8,128)(2,1)S(1)}, bf16[464,128]{1,0:T(8,128)(2,1)S(1)}, u32[]{:S(2)}, u32[]{:S(2)}) collective-permute-start(bf16[464,128]{1,0:T(8,128)(2,1)S(1)} %add.30), channel_id=1, source_target_pairs={{0,4},{1,5},{2,6},{3,7},{4,0},{5,1},{6,2},{7,3},{8,12},{9,13},{10,... | collective-permute-start | bytes 356360 | tf_op jit(solution)/shard_map/ppermute | solution.py:559
  36.7 11.8 %collective-permute-start.6 = (bf16[912,128]{1,0:T(8,128)(2,1)S(1)}, bf16[912,128]{1,0:T(8,128)(2,1)S(1)}, u32[]{:S(2)}, u32[]{:S(2)}) collective-permute-start(bf16[912,128]{1,0:T(8,128)(2,1)S(1)} %add.32), channel_id=1, source_target_pairs={{0,4},{1,5},{2,6},{3,7},{4,0},{5,1},{6,2},{7,3},{8,12},{9,13},{10,... | collective-permute-start | bytes 700424 | tf_op jit(solution)/shard_map/ppermute | solution.py:559
  38.0 10.7 %collective-permute-start.5 = (bf16[464,128]{1,0:T(8,128)(2,1)S(1)}, bf16[464,128]{1,0:T(8,128)(2,1)S(1)}, u32[]{:S(2)}, u32[]{:S(2)}) collective-permute-start(bf16[464,128]{1,0:T(8,128)(2,1)S(1)} %add.31.mine.mine1), channel_id=1, source_target_pairs={{0,2},{1,3},{2,0},{3,1},{4,6},{5,7},{6,4},{7,5},{8,10},{9,11},{10,... | collective-permute-start | bytes 356360 | tf_op jit(solution)/shard_map/ppermute | solution.py:559
  39.9 1.2 %copy-start.2 = (bf16[4,512,256]{2,1,0:T(8,128)(2,1)S(1)}, bf16[4,512,256]{2,1,0:T(8,128)(2,1)}, u32[]{:S(2)}) copy-start(bf16[4,512,256]{2,1,0:T(8,128)(2,1)} %leaf_input.1) | copy-start | bytes 3145732
  41.2 7.6 %copy-start.12 = (f32[256]{0:T(256)S(1)}, f32[256]{0:T(256)}, u32[]{:S(2)}) copy-start(f32[256]{0:T(256)} %param.28) | copy-start | bytes 3076
  48.6 7.7 %copy-start.1 = (bf16[2,512,512]{2,1,0:T(8,128)(2,1)S(1)}, bf16[2,512,512]{2,1,0:T(8,128)(2,1)}, u32[]{:S(2)}) copy-start(bf16[2,512,512]{2,1,0:T(8,128)(2,1)} %up_state_hbm.3) | copy-start | bytes 3145732
  48.7 7.7 %copy-start.4 = (bf16[2,512,256]{2,1,0:T(8,128)(2,1)S(1)}, bf16[2,512,256]{2,1,0:T(8,128)(2,1)}, u32[]{:S(2)}) copy-start(bf16[2,512,256]{2,1,0:T(8,128)(2,1)} %up_input_hbm.3) | copy-start | bytes 1572868
  48.7 7.7 %copy-start.10 = (f32[512]{0:T(512)S(1)}, f32[512]{0:T(512)}, u32[]{:S(2)}) copy-start(f32[512]{0:T(512)} %param.27) | copy-start | bytes 6148
  48.7 7.7 %copy-start.13 = (f32[2]{0:T(128)S(1)}, f32[2]{0:T(128)}, u32[]{:S(2)}) copy-start(f32[2]{0:T(128)} %up_weight) | copy-start | bytes 28
  48.7 7.7 %collective-permute-start.7 = (bf16[912,128]{1,0:T(8,128)(2,1)S(1)}, bf16[912,128]{1,0:T(8,128)(2,1)S(1)}, u32[]{:S(2)}, u32[]{:S(2)}) collective-permute-start(bf16[912,128]{1,0:T(8,128)(2,1)S(1)} %add.33.mine2), channel_id=1, source_target_pairs={{0,2},{1,3},{2,0},{3,1},{4,6},{5,7},{6,4},{7,5},{8,10},{9,11},{10,... | collective-permute-start | bytes 700424 | tf_op jit(solution)/shard_map/ppermute | solution.py:559
  59.7 1.4 %collective-permute-start.8 = (bf16[464,128]{1,0:T(8,128)(2,1)S(1)}, bf16[464,128]{1,0:T(8,128)(2,1)S(1)}, u32[]{:S(2)}, u32[]{:S(2)}) collective-permute-start(bf16[464,128]{1,0:T(8,128)(2,1)S(1)} %select_bitcast_fusion.1), channel_id=1, source_target_pairs={{0,1},{1,0},{2,3},{3,2},{4,5},{5,4},{6,7},{7,6},{8,9},{9,8},{10,11... | collective-permute-start | bytes 356360 | tf_op jit(solution)/shard_map/ppermute | solution.py:559
  59.8 2.4 %collective-permute-start.10 = (bf16[912,128]{1,0:T(8,128)(2,1)S(1)}, bf16[912,128]{1,0:T(8,128)(2,1)S(1)}, u32[]{:S(2)}, u32[]{:S(2)}) collective-permute-start(bf16[912,128]{1,0:T(8,128)(2,1)S(1)} %select_bitcast_fusion), channel_id=1, source_target_pairs={{0,1},{1,0},{2,3},{3,2},{4,5},{5,4},{6,7},{7,6},{8,9},{9,8},{10,11... | collective-permute-start | bytes 700424 | tf_op jit(solution)/shard_map/ppermute | solution.py:559
  61.1 4.9 %collective-permute-start.9 = (bf16[464,128]{1,0:T(8,128)(2,1)S(1)}, bf16[464,128]{1,0:T(8,128)(2,1)S(1)}, u32[]{:S(2)}, u32[]{:S(2)}) collective-permute-start(bf16[464,128]{1,0:T(8,128)(2,1)S(1)} %bitcast_add_fusion.1), channel_id=1, source_target_pairs={{0,8},{1,17},{2,10},{3,19},{4,12},{5,21},{6,14},{7,23},{8,0},{9,25... | collective-permute-start | bytes 356360 | tf_op jit(solution)/shard_map/ppermute | solution.py:627
  66.0 7.3 %collective-permute-start.13 = (bf16[912,128]{1,0:T(8,128)(2,1)S(1)}, bf16[912,128]{1,0:T(8,128)(2,1)S(1)}, u32[]{:S(2)}, u32[]{:S(2)}) collective-permute-start(bf16[912,128]{1,0:T(8,128)(2,1)S(1)} %bitcast_add_fusion), channel_id=1, source_target_pairs={{0,8},{1,17},{2,10},{3,19},{4,12},{5,21},{6,14},{7,23},{8,0},{9,25... | collective-permute-start | bytes 700424 | tf_op jit(solution)/shard_map/ppermute | solution.py:627
  67.0 7.1 %collective-permute-start.11 = (bf16[464,128]{1,0:T(8,128)(2,1)S(1)}, bf16[464,128]{1,0:T(8,128)(2,1)S(1)}, u32[]{:S(2)}, u32[]{:S(2)}) collective-permute-start(bf16[464,128]{1,0:T(8,128)(2,1)S(1)} %add.36), channel_id=1, source_target_pairs={{0,16},{1,9},{2,18},{3,11},{4,20},{5,13},{6,22},{7,15},{8,24},{9,1... | collective-permute-start | bytes 356360 | tf_op jit(solution)/shard_map/ppermute | solution.py:627
  73.4 6.1 %collective-permute-start.14 = (bf16[912,128]{1,0:T(8,128)(2,1)S(1)}, bf16[912,128]{1,0:T(8,128)(2,1)S(1)}, u32[]{:S(2)}, u32[]{:S(2)}) collective-permute-start(bf16[912,128]{1,0:T(8,128)(2,1)S(1)} %add.38), channel_id=1, source_target_pairs={{0,16},{1,9},{2,18},{3,11},{4,20},{5,13},{6,22},{7,15},{8,24},{9,1... | collective-permute-start | bytes 700424 | tf_op jit(solution)/shard_map/ppermute | solution.py:627
  74.2 5.5 %collective-permute-start.12 = (bf16[464,128]{1,0:T(8,128)(2,1)S(1)}, bf16[464,128]{1,0:T(8,128)(2,1)S(1)}, u32[]{:S(2)}, u32[]{:S(2)}) collective-permute-start(bf16[464,128]{1,0:T(8,128)(2,1)S(1)} %add.37.mine.mine1), channel_id=1, source_target_pairs={{0,1},{1,0},{2,3},{3,2},{4,5},{5,4},{6,7},{7,6},{8,9},{9,8},{10,11... | collective-permute-start | bytes 356360 | tf_op jit(solution)/shard_map/ppermute | solution.py:559
  74.3 11.8 %collective-permute-start.17 = (bf16[512,512]{1,0:T(8,128)(2,1)S(1)}, bf16[512,512]{1,0:T(8,128)(2,1)S(1)}, u32[]{:S(2)}, u32[]{:S(2)}) collective-permute-start(bf16[512,512]{1,0:T(8,128)(2,1)S(1)} %get-tuple-element.69.value_own), channel_id=1, source_target_pairs={{0,1},{1,0},{2,3},{3,2},{4,5},{5,4},{6,7},{7,6},{8,9},{9,8},{10,11... | collective-permute-start | bytes 1572872 | tf_op jit(solution)/shard_map/ppermute | solution.py:559
  74.8 11.3 %collective-permute-start.16 = (bf16[256,512]{1,0:T(8,128)(2,1)S(1)}, bf16[256,512]{1,0:T(8,128)(2,1)S(1)}, u32[]{:S(2)}, u32[]{:S(2)}) collective-permute-start(bf16[256,512]{1,0:T(8,128)(2,1)S(1)} %get-tuple-element.68.gain_own), channel_id=1, source_target_pairs={{0,1},{1,0},{2,3},{3,2},{4,5},{5,4},{6,7},{7,6},{8,9},{9,8},{10,11... | collective-permute-start | bytes 786440 | tf_op jit(solution)/shard_map/ppermute | solution.py:559
  79.6 6.5 %copy-start.3 = (bf16[1,512,512]{2,1,0:T(8,128)(2,1)S(1)}, bf16[1,512,512]{2,1,0:T(8,128)(2,1)}, u32[]{:S(2)}) copy-start(bf16[1,512,512]{2,1,0:T(8,128)(2,1)} %mid_state_hbm.3) | copy-start | bytes 1572868
  79.6 6.5 %copy-start.5 = (bf16[1,512,256]{2,1,0:T(8,128)(2,1)S(1)}, bf16[1,512,256]{2,1,0:T(8,128)(2,1)}, u32[]{:S(2)}) copy-start(bf16[1,512,256]{2,1,0:T(8,128)(2,1)} %mid_input_hbm.3) | copy-start | bytes 786436
  79.6 6.5 %copy-start.6 = (bf16[512,512]{1,0:T(8,128)(2,1)S(1)}, bf16[512,512]{1,0:T(8,128)(2,1)}, u32[]{:S(2)}) copy-start(bf16[512,512]{1,0:T(8,128)(2,1)} %root_cov_hbm.1) | copy-start | bytes 1572868
  79.6 6.5 %copy-start.11 = (f32[512]{0:T(512)S(1)}, f32[512]{0:T(512)}, u32[]{:S(2)}) copy-start(f32[512]{0:T(512)} %param.29) | copy-start | bytes 6148
  79.7 6.5 %collective-permute-start.15 = (bf16[912,128]{1,0:T(8,128)(2,1)S(1)}, bf16[912,128]{1,0:T(8,128)(2,1)S(1)}, u32[]{:S(2)}, u32[]{:S(2)}) collective-permute-start(bf16[912,128]{1,0:T(8,128)(2,1)S(1)} %add.39.mine2), channel_id=1, source_target_pairs={{0,1},{1,0},{2,3},{3,2},{4,5},{5,4},{6,7},{7,6},{8,9},{9,8},{10,11... | collective-permute-start | bytes 700424 | tf_op jit(solution)/shard_map/ppermute | solution.py:559

commit v2 on v1

--- a/solution.py
+++ b/solution.py
@@ -17,12 +17,10 @@
 f32 = jnp.float32
 bf16 = jnp.bfloat16
 
-FIRST = (
-    ("bb", 0, 0), ("bb", 1, 0), ("bb", 1, 1), ("ba", 0, 0), ("ba", 0, 1), ("ba", 0, 2), ("ba", 0, 3),
+FIRST = (("bb", 0, 0), ("bb", 1, 0), ("bb", 1, 1)) + tuple(
+    ("ba", i, j) for i in range(2) for j in range(4)
 )
-SECOND = tuple(("ba", 1, j) for j in range(4)) + tuple(
-    ("aa", i, j) for i in range(4) for j in range(i + 1)
-)
+SECOND = tuple(("aa", i, j) for i in range(4) for j in range(i + 1))
 PLACE = {name: (chunk, n) for chunk, names in enumerate((FIRST, SECOND)) for n, name in enumerate(names)}
 ROWS = (len(FIRST) * HT + WROWS, len(SECOND) * HT + WROWS)
 
@@ -346,7 +344,7 @@
 def upper_kernel(
     up_weight, mine1, other1, mine2, other2, inv_a, through, inv_s, scale,
     up_state_hbm, up_input_hbm, state_cost,
-    gain, value, out1, out2,
+    gain, value, out,
     up_state, up_input, sems, applied,
 ):
     _, core, half = place_in_col()
@@ -364,7 +362,7 @@
         lower_terms(up_state, up_input, applied),
         weight,
         spread_weight(weight, lax.axis_index("row") * S1_ROW + core, core),
-        (out1, out2),
+        (out.at[:, : ROWS[0], :], out.at[:, ROWS[0] :, :]),
     )
 
 
@@ -380,12 +378,12 @@
 
 
 def root_kernel(
-    count, parent, mine1, other1, mine2, other2, inv_a, through, inv_s, scale,
-    state_cost, noise_cov, gain_own, gain_other, value_own, value_other, root_cov_hbm,
+    count, parent, mine, other, state_cost, control_cost, noise_cov, gain_own, gain_other, value_own, value_other, root_cov_hbm,
     up_state_hbm, up_input_hbm, mid_state_hbm, mid_input_hbm, closed_leaf_hbm,
     gain_out, value_out, up_gain, up_value, up_cov_out, mid_cov_out, leaf_cov_out,
     gain, value, root_cov, up_state, up_input, mid_state, mid_input, closed_leaf, parent_gain,
     up_cov, mid_cov, leaf_cov, closed, moved, in_sems, leaf_sems, out_sems, leaf_out_sems,
+    inv_a, through, schur, inv_s, scale,
 ):
     _, core, _ = place_in_col()
     slots = closed_leaf.shape[0]
@@ -418,6 +416,9 @@
         mine_is_parent, gain_own[...].astype(f32), gain_other[...].astype(f32)
     ).astype(bf16)
 
+    mine1, mine2 = mine.at[: ROWS[0], :], mine.at[ROWS[0] :, :]
+    other1, other2 = other.at[: ROWS[0], :], other.at[ROWS[0] :, :]
+    solve_kernel(True, mine1, other1, control_cost, inv_a, through, inv_s, scale, schur)
     finish_packed(
         core, (mine1, other1, mine2, other2), (inv_a, through, inv_s, scale), state_cost, gain, value
     )
@@ -578,7 +579,6 @@
 
     (kept1, sent1), (kept2, sent2) = (local_sum(x) for x in packed)
     came1 = across(sent1, 2)
-    came1, sent2 = lax.optimization_barrier((came1, sent2))
     came2 = across(sent2, 2)
     came2, gain_then = lax.optimization_barrier((came2, mid_gain))
     closed_leaf = pl.pallas_call(
@@ -602,11 +602,11 @@
     solved = solve(False, first, control_rows)
     up_weight, closed_leaf = lax.optimization_barrier((up_weight, closed_leaf))
 
-    up_gain_own, up_value_own, *packed = pl.pallas_call(
+    up_gain_own, up_value_own, packed = pl.pallas_call(
         upper_kernel,
-        out_shape=(matrix(NU, NX), matrix(NX, NX), *PACKED),
+        out_shape=(matrix(NU, NX), matrix(NX, NX), matrix(2, sum(ROWS), T)),
         in_specs=[SMEM] + [VMEM] * 8 + [HBM] * 2 + [VMEM],
-        out_specs=(VMEM,) * 4,
+        out_specs=(VMEM,) * 3,
         scratch_shapes=[
             pltpu.VMEM((NX, NX), bf16),
             pltpu.VMEM((NX, NU), bf16),
@@ -634,22 +634,11 @@
             ],
         )
 
-    def chip_sum(x):
-        sent = jnp.where(is_low, x[1], x[0])
-        return jnp.where(is_low, x[0], x[1]) + across(sent, 1)
-
-    def rest_of_row(kept):
-        for step in range(1, row_bits):
-            kept = kept + along(kept, step)
-        return kept, across(kept, 1)
-
-    kept1, kept2 = (chip_sum(x) for x in packed)
-    came1 = along(kept1, 0)
-    came1, kept2 = lax.optimization_barrier((came1, kept2))
-    came2 = along(kept2, 0)
-    first = rest_of_row(kept1 + came1)
-    second = rest_of_row(kept2 + came2)
-    solved = solve(True, first, control_rows)
+    kept = jnp.where(is_low, packed[0], packed[1]) + across(
+        jnp.where(is_low, packed[1], packed[0]), 1
+    )
+    for step in range(row_bits):
+        kept = kept + along(kept, step)
 
     root_gain, root_value, up_gain, up_value, up_cov, mid_cov, leaf_cov = pl.pallas_call(
         root_kernel,
@@ -662,7 +651,7 @@
             matrix(1, NX, NX),
             matrix(slots, NX, NX),
         ),
-        in_specs=[SMEM] * 2 + [VMEM] * 14 + [HBM] * 6,
+        in_specs=[SMEM] * 2 + [VMEM] * 9 + [HBM] * 6,
         out_specs=(HBM,) * 7,
         scratch_shapes=[
             pltpu.VMEM((NU, NX), bf16),
@@ -683,16 +672,18 @@
             DMA((slots,)),
             DMA((8,)),
             DMA((slots,)),
+            *SQUARES,
+            pltpu.VMEM((HT, T), f32),
         ],
         compiler_params=limit(32),
         name="root",
     )(
         leaf_count,
         mid_parent,
-        *first,
-        *second,
-        *solved,
+        kept,
+        across(kept, 1),
         state_rows,
+        control_rows,
         noise_rows,
         up_gain_own,
         up_gain_other,

time: 96.7 us -> 96.1 us (level)
  starting transfers between devices: 15.6 us -> 11.5 us
  waiting for transfers between devices: 32.1 us -> 35.6 us
    pallas_call x2 -> x1, Pallas kernels: 12.7 us -> 6.37 us  [solve(): pl.pallas_call(functools.partial(solve_kernel, by_core), out_shape=(squar...]
    pallas_call x1, Pallas kernels: 10.3 us -> 16.4 us  [local(): pl.pallas_call(root_kernel, out_shape=(matrix(NU, NX), matrix(NX, NX), ma...]
    ppermute x14 -> x12, waiting for transfers between devices: 18.8 us -> 24 us  [across(): return lax.ppermute(x, 'col', [(i, i ^ flip) for i in range(n_col)])]
    ppermute x14 -> x12, starting transfers between devices: 11.4 us -> 8.57 us  [across(): return lax.ppermute(x, 'col', [(i, i ^ flip) for i in range(n_col)])]
    ppermute x4 -> x2, waiting for transfers between devices: 13.3 us -> 11.6 us  [along(): lax.ppermute(x, ('row', 'col'), [(r * n_col + c, (r ^ 1 << bits[c % 2]) *...]
    ppermute x4 -> x2, starting transfers between devices: 4.23 us -> 2.95 us  [along(): lax.ppermute(x, ('row', 'col'), [(r * n_col + c, (r ^ 1 << bits[c % 2]) *...]
  transfers between devices with their start and end apart: 18 -> 14, of which waited for: 9 -> 9; matrix products, arithmetic and copies ran while one was open for 1% -> 0% of each run, Pallas kernels for 15% -> 8%
where the time goes in v2:
time: 96.1 us; the launch traced here: 96.6 us
  Pallas kernels  41.8 us (43%)
  waiting for transfers between devices  35.6 us (37%)
  starting transfers between devices  11.5 us (12%)
  local copies, waits for them, and re-layouts  4.2 us (4%)
  between operations  3.02 us (3%)
    ppermute x12, waiting for transfers between devices, across(): return lax.ppermute(x, 'col', [(i, i ^ flip) for i in range(n_col)])  24 us
    pallas_call x1, Pallas kernels, local(): pl.pallas_call(root_kernel, out_shape=(matrix(NU, NX), matrix(NX, NX), ma...  16.4 us
    pallas_call x1, Pallas kernels, local(): pl.pallas_call(lower_kernel, out_shape=(matrix(NU, NX), matrix(NX, NX), *...  14.1 us
    ppermute x2, waiting for transfers between devices, along(): lax.ppermute(x, ('row', 'col'), [(r * n_col + c, (r ^ 1 << bits[c % 2]) *...  11.6 us
    ppermute x12, starting transfers between devices, across(): return lax.ppermute(x, 'col', [(i, i ^ flip) for i in range(n_col)])  8.57 us
    pallas_call x1, Pallas kernels, solve(): pl.pallas_call(functools.partial(solve_kernel, by_core), out_shape=(squar...  6.37 us
    unnamed x28, local copies, waits for them, and re-layouts  4.2 us
    pallas_call x1, Pallas kernels, local(): pl.pallas_call(upper_kernel, out_shape=(matrix(NU, NX), matrix(NX, NX), m...  3.27 us
  transfers between devices with their start and end apart: 14, of which 9 were waited for; matrix products, arithmetic and copies ran while one was open for 0% of the time, Pallas kernels for 8%

profile of v2, /device:TPU:0, one launch (start us, length us, event | category | flops | bytes accessed | tf_op | source)
XLA Modules:
  0.0 96.6 jit_solution(1296154899471864964)
XLA Ops:
  2.6 14.1 %lower.1 = (bf16[256,512]{1,0:T(8,128)(2,1)}, bf16[512,512]{1,0:T(8,128)(2,1)}, bf16[2,720,128]{2,1,0:T(8,128)(2,1)}, bf16[2,656,128]{2,1,0:T(8,128)(2,1)}) custom-call(s32[1]{0:T(128)S(6)} %copy.24.count, f32[1]{0:T(128)S(6)} %copy.25.mid_weight, s32[1]{0:T(128)S(6)} %copy.26.parent, bf16[1,4]{1,0:T(2,128)(2,1)} %bitcast.18, ...), custom_call_target="tpu_custom_call" | custom-call | tf_op jit(solution)/shard_map/lower/pallas_call | solution.py:525
  16.7 0.0 copy-start
  16.7 0.6 collective-permute-start.2
  17.3 0.1 collective-permute-start
  17.4 1.4 %collective-permute-done.2.came = bf16[2,720,128]{2,1,0:T(8,128)(2,1)S(1)} collective-permute-done((bf16[2,720,128]{2,1,0:T(8,128)(2,1)}, bf16[2,720,128]{2,1,0:T(8,128)(2,1)S(1)}, u32[]{:S(2)}, u32[]{:S(2)}) %collective-permute-start.2) | collective-permute-done | bytes 368672 | tf_op jit(solution)/shard_map/ppermute | solution.py:560
  18.8 0.0 copy-start.7
  18.8 1.0 %copy-done.7 = bf16[2,720,128]{2,1,0:T(8,128)(2,1)S(1)} copy-done((bf16[2,720,128]{2,1,0:T(8,128)(2,1)S(1)}, bf16[2,720,128]{2,1,0:T(8,128)(2,1)}, u32[]{:S(2)}) %copy-start.7) | copy-done | bytes 368664
  19.8 0.2 local_sum.3
  20.0 1.6 %collective-permute-start.3 = (bf16[720,128]{1,0:T(8,128)(2,1)S(1)}, bf16[720,128]{1,0:T(8,128)(2,1)S(1)}, u32[]{:S(2)}, u32[]{:S(2)}) collective-permute-start(bf16[720,128]{1,0:T(8,128)(2,1)S(1)} %get-tuple-element.42), channel_id=1, source_target_pairs={{0,2},{1,3},{2,0},{3,1},{4,6},{5,7},{6,4},{7,5},{8,10},{9,11},{10,... | collective-permute-start | bytes 552968 | tf_op jit(solution)/shard_map/ppermute | solution.py:560
  21.6 5.4 %collective-permute-done.3 = bf16[720,128]{1,0:T(8,128)(2,1)S(1)} collective-permute-done((bf16[720,128]{1,0:T(8,128)(2,1)S(1)}, bf16[720,128]{1,0:T(8,128)(2,1)S(1)}, u32[]{:S(2)}, u32[]{:S(2)}) %collective-permute-start.3) | collective-permute-done | bytes 184352 | tf_op jit(solution)/shard_map/ppermute | solution.py:560
  27.0 0.1 add.21
  27.1 3.8 %collective-permute-start.4 = (bf16[720,128]{1,0:T(8,128)(2,1)S(1)}, bf16[720,128]{1,0:T(8,128)(2,1)S(1)}, u32[]{:S(2)}, u32[]{:S(2)}) collective-permute-start(bf16[720,128]{1,0:T(8,128)(2,1)S(1)} %add.21), channel_id=1, source_target_pairs={{0,4},{1,5},{2,6},{3,7},{4,0},{5,1},{6,2},{7,3},{8,12},{9,13},{10,... | collective-permute-start | bytes 552968 | tf_op jit(solution)/shard_map/ppermute | solution.py:560
  30.9 0.0 collective-permute-done.came
  30.9 1.0 %copy-done.8 = bf16[2,656,128]{2,1,0:T(8,128)(2,1)S(1)} copy-done((bf16[2,656,128]{2,1,0:T(8,128)(2,1)S(1)}, bf16[2,656,128]{2,1,0:T(8,128)(2,1)}, u32[]{:S(2)}) %copy-start.8) | copy-done | bytes 335896
  31.8 0.2 local_sum.2
  32.1 0.4 collective-permute-start.1
  32.4 6.6 %collective-permute-done.4 = bf16[720,128]{1,0:T(8,128)(2,1)S(1)} collective-permute-done((bf16[720,128]{1,0:T(8,128)(2,1)S(1)}, bf16[720,128]{1,0:T(8,128)(2,1)S(1)}, u32[]{:S(2)}, u32[]{:S(2)}) %collective-permute-start.4) | collective-permute-done | bytes 184352 | tf_op jit(solution)/shard_map/ppermute | solution.py:560
  39.0 0.1 add.22.mine.mine1
  39.0 0.1 collective-permute-start.5
  39.1 2.0 %collective-permute-done.1 = bf16[656,128]{1,0:T(8,128)(2,1)S(1)} collective-permute-done((bf16[656,128]{1,0:T(8,128)(2,1)S(1)}, bf16[656,128]{1,0:T(8,128)(2,1)S(1)}, u32[]{:S(2)}, u32[]{:S(2)}) %collective-permute-start.1) | collective-permute-done | bytes 167968 | tf_op jit(solution)/shard_map/ppermute | solution.py:560
  41.2 1.1 %collective-permute-start.6 = (bf16[656,128]{1,0:T(8,128)(2,1)S(1)}, bf16[656,128]{1,0:T(8,128)(2,1)S(1)}, u32[]{:S(2)}, u32[]{:S(2)}) collective-permute-start(bf16[656,128]{1,0:T(8,128)(2,1)S(1)} %add.23), channel_id=1, source_target_pairs={{0,4},{1,5},{2,6},{3,7},{4,0},{5,1},{6,2},{7,3},{8,12},{9,13},{10,... | collective-permute-start | bytes 503816 | tf_op jit(solution)/shard_map/ppermute | solution.py:560
  42.3 0.0 copy-done
  42.3 1.2 %copy-done.1 = bf16[4,512,256]{2,1,0:T(8,128)(2,1)S(1)} copy-done((bf16[4,512,256]{2,1,0:T(8,128)(2,1)S(1)}, bf16[4,512,256]{2,1,0:T(8,128)(2,1)}, u32[]{:S(2)}) %copy-start.1) | copy-done | bytes 1048600
  43.6 0.9 copy-done.9
  44.5 1.2 %close.1.closed_leaf_hbm = bf16[4,512,512]{2,1,0:T(8,128)(2,1)S(1)} custom-call(bf16[4,512,512]{2,1,0:T(8,128)(2,1)S(1)} %copy-done, bf16[4,512,256]{2,1,0:T(8,128)(2,1)S(1)} %copy-done.1, bf16[256,512]{1,0:T(8,128)(2,1)S(1)} %copy-done.9), custom_call_target="tpu_custom_call" | custom-call | flops 536870912 | bytes 5242880 | tf_op jit(solution)/shard_map/close/pallas_call | solution.py:584
  45.7 5.4 %collective-permute-done.6 = bf16[656,128]{1,0:T(8,128)(2,1)S(1)} collective-permute-done((bf16[656,128]{1,0:T(8,128)(2,1)S(1)}, bf16[656,128]{1,0:T(8,128)(2,1)S(1)}, u32[]{:S(2)}, u32[]{:S(2)}) %collective-permute-start.6) | collective-permute-done | bytes 167968 | tf_op jit(solution)/shard_map/ppermute | solution.py:560
  51.1 0.0 copy-start.2
  51.1 0.0 copy-start.4
  51.2 0.0 copy-start.10
  51.2 0.0 copy-start.13
  51.2 0.1 collective-permute-start.7
  51.3 0.0 collective-permute-done.5.other.other1
  51.3 0.0 copy-done.11
  51.3 6.4 %solve.1 = (f32[128,128]{1,0:T(8,128)S(1)}, f32[128,128]{1,0:T(8,128)S(1)}, f32[128,128]{1,0:T(8,128)S(1)}, f32[64,128]{1,0:T(8,128)S(1)}) custom-call(bf16[720,128]{1,0:T(8,128)(2,1)S(1)} %add.22.mine.mine1, bf16[720,128]{1,0:T(8,128)(2,1)S(1)} %collective-permute-done.5.other.other1, f32[2,128]{1,0:T(2,128)S(1)} %bitcast.15), custom_call_target="tpu_custom_call" | custom-call | flops 5000000000 | bytes 262144 | tf_op jit(solution)/shard_map/solve/pallas_call | solution.py:488
  57.7 0.0 collective-permute-done.7.other2
  57.7 0.0 copy-done.2
  57.7 0.0 copy-done.4
  57.7 0.0 copy-done.10
  57.7 0.0 copy-done.13
  57.7 3.3 %upper.1 = (bf16[256,512]{1,0:T(8,128)(2,1)S(1)}, bf16[512,512]{1,0:T(8,128)(2,1)S(1)}, bf16[2,1376,128]{2,1,0:T(8,128)(2,1)S(1)}) custom-call(f32[2]{0:T(128)S(1)} %copy-done.13, bf16[720,128]{1,0:T(8,128)(2,1)S(1)} %add.22.mine.mine1, bf16[720,128]{1,0:T(8,128)(2,1)S(1)} %collective-permute-done.5.other.other1, bf16[656,128]{1,0:T(8,128)(2,1)S(1)} %add.24.mine2, ...), custom_call_target="tpu_custom_call" | custom-call | tf_op jit(solution)/shard_map/upper/pallas_call | solution.py:605
  61.0 0.0 copy-start.3
  61.0 0.0 copy-start.5
  61.0 0.0 copy-start.6
  61.0 0.0 copy-start.12
  61.1 0.1 collective-permute-start.8
  61.2 1.7 %collective-permute-done.8 = bf16[1376,128]{1,0:T(8,128)(2,1)S(1)} collective-permute-done((bf16[1376,128]{1,0:T(8,128)(2,1)S(1)}, bf16[1376,128]{1,0:T(8,128)(2,1)S(1)}, u32[]{:S(2)}, u32[]{:S(2)}) %collective-permute-start.8) | collective-permute-done | bytes 352288 | tf_op jit(solution)/shard_map/ppermute | solution.py:560
  62.8 0.1 bitcast_add_fusion
  62.9 2.2 %collective-permute-start.9 = (bf16[1376,128]{1,0:T(8,128)(2,1)S(1)}, bf16[1376,128]{1,0:T(8,128)(2,1)S(1)}, u32[]{:S(2)}, u32[]{:S(2)}) collective-permute-start(bf16[1376,128]{1,0:T(8,128)(2,1)S(1)} %bitcast_add_fusion), channel_id=1, source_target_pairs={{0,8},{1,17},{2,10},{3,19},{4,12},{5,21},{6,14},{7,23},{8,0},{9,25... | collective-permute-start | bytes 1056776 | tf_op jit(solution)/shard_map/ppermute | solution.py:627
  65.0 5.3 %collective-permute-done.9 = bf16[1376,128]{1,0:T(8,128)(2,1)S(1)} collective-permute-done((bf16[1376,128]{1,0:T(8,128)(2,1)S(1)}, bf16[1376,128]{1,0:T(8,128)(2,1)S(1)}, u32[]{:S(2)}, u32[]{:S(2)}) %collective-permute-start.9) | collective-permute-done | bytes 352288 | tf_op jit(solution)/shard_map/ppermute | solution.py:627
  70.4 0.1 add.26
  70.5 0.8 collective-permute-start.10
  71.2 0.3 collective-permute-start.13
  71.5 6.3 %collective-permute-done.10 = bf16[1376,128]{1,0:T(8,128)(2,1)S(1)} collective-permute-done((bf16[1376,128]{1,0:T(8,128)(2,1)S(1)}, bf16[1376,128]{1,0:T(8,128)(2,1)S(1)}, u32[]{:S(2)}, u32[]{:S(2)}) %collective-permute-start.10) | collective-permute-done | bytes 352288 | tf_op jit(solution)/shard_map/ppermute | solution.py:627
  77.9 0.1 add.27.mine
  78.0 0.1 collective-permute-start.11
  78.0 0.5 collective-permute-start.12
  78.5 1.5 %collective-permute-done.12.gain_other = bf16[256,512]{1,0:T(8,128)(2,1)S(1)} collective-permute-done((bf16[256,512]{1,0:T(8,128)(2,1)S(1)}, bf16[256,512]{1,0:T(8,128)(2,1)S(1)}, u32[]{:S(2)}, u32[]{:S(2)}) %collective-permute-start.12) | collective-permute-done | bytes 262176 | tf_op jit(solution)/shard_map/ppermute | solution.py:560
  80.1 0.0 collective-permute-done.13.value_other
  80.1 0.0 collective-permute-done.11.other
  80.1 0.0 copy-done.3
  80.1 0.0 copy-done.5
  80.1 0.0 copy-done.6
  80.1 0.0 copy-done.12
  80.1 16.4 %root.1 = (bf16[256,512]{1,0:T(8,128)(2,1)}, bf16[512,512]{1,0:T(8,128)(2,1)}, bf16[2,256,512]{2,1,0:T(8,128)(2,1)}, bf16[2,512,512]{2,1,0:T(8,128)(2,1)}, bf16[...) custom-call(s32[1]{0:T(128)S(6)} %copy.24.count, s32[1]{0:T(128)S(6)} %copy.26.parent, ...), custom_call_target="tpu_custom_call" | custom-call | tf_op jit(solution)/shard_map/root/pallas_call | solution.py:643
  (7 shorter events, 0.1 us)
Async XLA Ops:
  16.7 25.6 %copy-start = (bf16[4,512,512]{2,1,0:T(8,128)(2,1)S(1)}, bf16[4,512,512]{2,1,0:T(8,128)(2,1)}, u32[]{:S(2)}) copy-start(bf16[4,512,512]{2,1,0:T(8,128)(2,1)} %leaf_state.1) | copy-start | bytes 6291460
  16.7 2.1 %collective-permute-start.2 = (bf16[2,720,128]{2,1,0:T(8,128)(2,1)}, bf16[2,720,128]{2,1,0:T(8,128)(2,1)S(1)}, u32[]{:S(2)}, u32[]{:S(2)}) collective-permute-start(bf16[2,720,128]{2,1,0:T(8,128)(2,1)} %get-tuple-element.40.mine), channel_id=1, source_target_pairs={{0,1},{1,0},{2,3},{3,2},{4,5},{5,4},{6,7},{7,6},{8,9},{9,8},{10,11... | collective-permute-start | bytes 1105928 | tf_op jit(solution)/shard_map/ppermute | solution.py:560
  17.3 13.6 %collective-permute-start = (bf16[2,656,128]{2,1,0:T(8,128)(2,1)}, bf16[2,656,128]{2,1,0:T(8,128)(2,1)S(1)}, u32[]{:S(2)}, u32[]{:S(2)}) collective-permute-start(bf16[2,656,128]{2,1,0:T(8,128)(2,1)} %get-tuple-element.35.mine), channel_id=1, source_target_pairs={{0,1},{1,0},{2,3},{3,2},{4,5},{5,4},{6,7},{7,6},{8,9},{9,8},{10,11... | collective-permute-start | bytes 1007624 | tf_op jit(solution)/shard_map/ppermute | solution.py:560
  18.8 1.0 %copy-start.7 = (bf16[2,720,128]{2,1,0:T(8,128)(2,1)S(1)}, bf16[2,720,128]{2,1,0:T(8,128)(2,1)}, u32[]{:S(2)}) copy-start(bf16[2,720,128]{2,1,0:T(8,128)(2,1)} %get-tuple-element.40.mine) | copy-start | bytes 1105924
  20.0 7.0 %collective-permute-start.3 = (bf16[720,128]{1,0:T(8,128)(2,1)S(1)}, bf16[720,128]{1,0:T(8,128)(2,1)S(1)}, u32[]{:S(2)}, u32[]{:S(2)}) collective-permute-start(bf16[720,128]{1,0:T(8,128)(2,1)S(1)} %get-tuple-element.42), channel_id=1, source_target_pairs={{0,2},{1,3},{2,0},{3,1},{4,6},{5,7},{6,4},{7,5},{8,10},{9,11},{10,... | collective-permute-start | bytes 552968 | tf_op jit(solution)/shard_map/ppermute | solution.py:560
  27.1 11.9 %collective-permute-start.4 = (bf16[720,128]{1,0:T(8,128)(2,1)S(1)}, bf16[720,128]{1,0:T(8,128)(2,1)S(1)}, u32[]{:S(2)}, u32[]{:S(2)}) collective-permute-start(bf16[720,128]{1,0:T(8,128)(2,1)S(1)} %add.21), channel_id=1, source_target_pairs={{0,4},{1,5},{2,6},{3,7},{4,0},{5,1},{6,2},{7,3},{8,12},{9,13},{10,... | collective-permute-start | bytes 552968 | tf_op jit(solution)/shard_map/ppermute | solution.py:560
  30.9 1.0 %copy-start.8 = (bf16[2,656,128]{2,1,0:T(8,128)(2,1)S(1)}, bf16[2,656,128]{2,1,0:T(8,128)(2,1)}, u32[]{:S(2)}) copy-start(bf16[2,656,128]{2,1,0:T(8,128)(2,1)} %get-tuple-element.35.mine) | copy-start | bytes 1007620
  32.1 9.1 %collective-permute-start.1 = (bf16[656,128]{1,0:T(8,128)(2,1)S(1)}, bf16[656,128]{1,0:T(8,128)(2,1)S(1)}, u32[]{:S(2)}, u32[]{:S(2)}) collective-permute-start(bf16[656,128]{1,0:T(8,128)(2,1)S(1)} %get-tuple-element.36), channel_id=1, source_target_pairs={{0,2},{1,3},{2,0},{3,1},{4,6},{5,7},{6,4},{7,5},{8,10},{9,11},{10,... | collective-permute-start | bytes 503816 | tf_op jit(solution)/shard_map/ppermute | solution.py:560
  39.0 12.2 %collective-permute-start.5 = (bf16[720,128]{1,0:T(8,128)(2,1)S(1)}, bf16[720,128]{1,0:T(8,128)(2,1)S(1)}, u32[]{:S(2)}, u32[]{:S(2)}) collective-permute-start(bf16[720,128]{1,0:T(8,128)(2,1)S(1)} %add.22.mine.mine1), channel_id=1, source_target_pairs={{0,2},{1,3},{2,0},{3,1},{4,6},{5,7},{6,4},{7,5},{8,10},{9,11},{10,... | collective-permute-start | bytes 552968 | tf_op jit(solution)/shard_map/ppermute | solution.py:560
  41.2 9.8 %collective-permute-start.6 = (bf16[656,128]{1,0:T(8,128)(2,1)S(1)}, bf16[656,128]{1,0:T(8,128)(2,1)S(1)}, u32[]{:S(2)}, u32[]{:S(2)}) collective-permute-start(bf16[656,128]{1,0:T(8,128)(2,1)S(1)} %add.23), channel_id=1, source_target_pairs={{0,4},{1,5},{2,6},{3,7},{4,0},{5,1},{6,2},{7,3},{8,12},{9,13},{10,... | collective-permute-start | bytes 503816 | tf_op jit(solution)/shard_map/ppermute | solution.py:560
  42.3 1.2 %copy-start.1 = (bf16[4,512,256]{2,1,0:T(8,128)(2,1)S(1)}, bf16[4,512,256]{2,1,0:T(8,128)(2,1)}, u32[]{:S(2)}) copy-start(bf16[4,512,256]{2,1,0:T(8,128)(2,1)} %leaf_input.1) | copy-start | bytes 3145732
  43.6 0.9 copy-start.9
  44.5 6.8 %copy-start.11 = (f32[256]{0:T(256)S(1)}, f32[256]{0:T(256)}, u32[]{:S(2)}) copy-start(f32[256]{0:T(256)} %param.28) | copy-start | bytes 3076
  51.1 6.5 %copy-start.2 = (bf16[2,512,512]{2,1,0:T(8,128)(2,1)S(1)}, bf16[2,512,512]{2,1,0:T(8,128)(2,1)}, u32[]{:S(2)}) copy-start(bf16[2,512,512]{2,1,0:T(8,128)(2,1)} %up_state_hbm.3) | copy-start | bytes 3145732
  51.1 6.5 %copy-start.4 = (bf16[2,512,256]{2,1,0:T(8,128)(2,1)S(1)}, bf16[2,512,256]{2,1,0:T(8,128)(2,1)}, u32[]{:S(2)}) copy-start(bf16[2,512,256]{2,1,0:T(8,128)(2,1)} %up_input_hbm.3) | copy-start | bytes 1572868
  51.2 6.5 %copy-start.10 = (f32[512]{0:T(512)S(1)}, f32[512]{0:T(512)}, u32[]{:S(2)}) copy-start(f32[512]{0:T(512)} %param.27) | copy-start | bytes 6148
  51.2 6.5 %copy-start.13 = (f32[2]{0:T(128)S(1)}, f32[2]{0:T(128)}, u32[]{:S(2)}) copy-start(f32[2]{0:T(128)} %up_weight) | copy-start | bytes 28
  51.2 6.5 %collective-permute-start.7 = (bf16[656,128]{1,0:T(8,128)(2,1)S(1)}, bf16[656,128]{1,0:T(8,128)(2,1)S(1)}, u32[]{:S(2)}, u32[]{:S(2)}) collective-permute-start(bf16[656,128]{1,0:T(8,128)(2,1)S(1)} %add.24.mine2), channel_id=1, source_target_pairs={{0,2},{1,3},{2,0},{3,1},{4,6},{5,7},{6,4},{7,5},{8,10},{9,11},{10,... | collective-permute-start | bytes 503816 | tf_op jit(solution)/shard_map/ppermute | solution.py:560
  61.0 19.1 %copy-start.3 = (bf16[1,512,512]{2,1,0:T(8,128)(2,1)S(1)}, bf16[1,512,512]{2,1,0:T(8,128)(2,1)}, u32[]{:S(2)}) copy-start(bf16[1,512,512]{2,1,0:T(8,128)(2,1)} %mid_state_hbm.3) | copy-start | bytes 1572868
  61.0 19.1 %copy-start.5 = (bf16[1,512,256]{2,1,0:T(8,128)(2,1)S(1)}, bf16[1,512,256]{2,1,0:T(8,128)(2,1)}, u32[]{:S(2)}) copy-start(bf16[1,512,256]{2,1,0:T(8,128)(2,1)} %mid_input_hbm.3) | copy-start | bytes 786436
  61.0 19.1 %copy-start.6 = (bf16[512,512]{1,0:T(8,128)(2,1)S(1)}, bf16[512,512]{1,0:T(8,128)(2,1)}, u32[]{:S(2)}) copy-start(bf16[512,512]{1,0:T(8,128)(2,1)} %root_cov_hbm.1) | copy-start | bytes 1572868
  61.0 19.1 %copy-start.12 = (f32[512]{0:T(512)S(1)}, f32[512]{0:T(512)}, u32[]{:S(2)}) copy-start(f32[512]{0:T(512)} %param.29) | copy-start | bytes 6148
  61.1 1.7 %collective-permute-start.8 = (bf16[1376,128]{1,0:T(8,128)(2,1)S(1)}, bf16[1376,128]{1,0:T(8,128)(2,1)S(1)}, u32[]{:S(2)}, u32[]{:S(2)}) collective-permute-start(bf16[1376,128]{1,0:T(8,128)(2,1)S(1)} %select_bitcast_fusion), channel_id=1, source_target_pairs={{0,1},{1,0},{2,3},{3,2},{4,5},{5,4},{6,7},{7,6},{8,9},{9,8},{10,11... | collective-permute-start | bytes 1056776 | tf_op jit(solution)/shard_map/ppermute | solution.py:560
  62.9 7.5 %collective-permute-start.9 = (bf16[1376,128]{1,0:T(8,128)(2,1)S(1)}, bf16[1376,128]{1,0:T(8,128)(2,1)S(1)}, u32[]{:S(2)}, u32[]{:S(2)}) collective-permute-start(bf16[1376,128]{1,0:T(8,128)(2,1)S(1)} %bitcast_add_fusion), channel_id=1, source_target_pairs={{0,8},{1,17},{2,10},{3,19},{4,12},{5,21},{6,14},{7,23},{8,0},{9,25... | collective-permute-start | bytes 1056776 | tf_op jit(solution)/shard_map/ppermute | solution.py:627
  70.5 7.4 %collective-permute-start.10 = (bf16[1376,128]{1,0:T(8,128)(2,1)S(1)}, bf16[1376,128]{1,0:T(8,128)(2,1)S(1)}, u32[]{:S(2)}, u32[]{:S(2)}) collective-permute-start(bf16[1376,128]{1,0:T(8,128)(2,1)S(1)} %add.26), channel_id=1, source_target_pairs={{0,16},{1,9},{2,18},{3,11},{4,20},{5,13},{6,22},{7,15},{8,24},{9,1... | collective-permute-start | bytes 1056776 | tf_op jit(solution)/shard_map/ppermute | solution.py:627
  71.2 8.8 %collective-permute-start.13 = (bf16[512,512]{1,0:T(8,128)(2,1)S(1)}, bf16[512,512]{1,0:T(8,128)(2,1)S(1)}, u32[]{:S(2)}, u32[]{:S(2)}) collective-permute-start(bf16[512,512]{1,0:T(8,128)(2,1)S(1)} %get-tuple-element.51.value_own), channel_id=1, source_target_pairs={{0,1},{1,0},{2,3},{3,2},{4,5},{5,4},{6,7},{7,6},{8,9},{9,8},{10,11... | collective-permute-start | bytes 1572872 | tf_op jit(solution)/shard_map/ppermute | solution.py:560
  78.0 2.1 %collective-permute-start.11 = (bf16[1376,128]{1,0:T(8,128)(2,1)S(1)}, bf16[1376,128]{1,0:T(8,128)(2,1)S(1)}, u32[]{:S(2)}, u32[]{:S(2)}) collective-permute-start(bf16[1376,128]{1,0:T(8,128)(2,1)S(1)} %add.27.mine), channel_id=1, source_target_pairs={{0,1},{1,0},{2,3},{3,2},{4,5},{5,4},{6,7},{7,6},{8,9},{9,8},{10,11... | collective-permute-start | bytes 1056776 | tf_op jit(solution)/shard_map/ppermute | solution.py:560
  78.0 2.0 %collective-permute-start.12 = (bf16[256,512]{1,0:T(8,128)(2,1)S(1)}, bf16[256,512]{1,0:T(8,128)(2,1)S(1)}, u32[]{:S(2)}, u32[]{:S(2)}) collective-permute-start(bf16[256,512]{1,0:T(8,128)(2,1)S(1)} %get-tuple-element.50.gain_own), channel_id=1, source_target_pairs={{0,1},{1,0},{2,3},{3,2},{4,5},{5,4},{6,7},{7,6},{8,9},{9,8},{10,11... | collective-permute-start | bytes 786440 | tf_op jit(solution)/shard_map/ppermute | solution.py:560
